TPU v7x, 512 devices: a whole 4x4x16 slice. The times are simulated.
512 devices in a mesh: band: 16 (over y_hi, x, core), tm: 32 (over y_lo, z).
Axes of the slice: x: 4, y: 4 (y_hi: 2, y_lo: 2; y = y_hi * 2 + y_lo), z: 16, core: 2. Of those that a mesh axis runs over, the one named last changes fastest.
Arguments:
- spectrum: bfloat16 [64, 128, 65536], P(None, 'band', 'tm'), may hold values from -6 to 6
- w_freq: bfloat16 [5, 64, 8], replicated, may hold values from -1 to 1
- b_freq: float32 [64], replicated, may hold values from -3 to 3
- dilation: int32 [64], replicated, may hold values from 1 to 128, as said below
- w_time: float32 [3, 64], replicated, may hold values from -3 to 3
- b_time: float32 [64], replicated, may hold values from -3 to 3
- w_mix: bfloat16 [128, 128], replicated, may hold values from -0.5 to 0.5
- ln_gain: float32 [64], replicated, may hold values from 0.1 to 1.9
- w_up: bfloat16 [64, 256], replicated, may hold values from -0.75 to 0.75
- b_up: float32 [256], replicated, may hold values from -3 to 3
- w_down: bfloat16 [256, 64], replicated, may hold values from -0.375 to 0.375
- b_down: float32 [64], replicated, may hold values from -3 to 3
- epoch_lengths: int32 [32, 8], P('tm'), may hold values from 1 to 1024, 2048 in all within a row
Outputs:
- epoch_mean: float32 [256, 8192], P('tm', 'band')
- epoch_power: float32 [256, 8192], P('tm', 'band')
Inputs may be any that keep to these rules, and one draw needn't show every extreme that they name: One channel has a dilation of exactly 128.
All inputs are finite; a program needn't handle non-finite values.
Results may differ from a plain program's by a relative error of at most 0.0015.
Values may be sent and summed in bfloat16 or wider, within the bound.
A program may use at most 64 MiB of HBM per device.

v0:
```python
import jax
import jax.numpy as jnp
from jax import lax
from jax.sharding import PartitionSpec as P


def padded_2(block, sides, width, periodic):
    for axis, dim in sides:
        count = lax.axis_size(axis)
        forward = [(i, i + 1) for i in range(count - 1)]
        if periodic:
            forward.append((count - 1, 0))
        backward = [(target, source) for source, target in forward]
        low = lax.ppermute(
            lax.slice_in_dim(block, block.shape[dim] - width, None, axis=dim), axis, forward
        )
        high = lax.ppermute(lax.slice_in_dim(block, 0, width, axis=dim), axis, backward)
        block = jnp.concatenate([low, block, high], axis=dim)
    return block


def dilated(ext, dilation, w_time, b_time, pad, length):

    def one(chan, step, taps, shift):
        left = lax.dynamic_slice_in_dim(chan, pad - step, length, 1).astype(jnp.float32)
        middle = chan[:, pad : pad + length].astype(jnp.float32)
        right = lax.dynamic_slice_in_dim(chan, pad + step, length, 1).astype(jnp.float32)
        return taps[0] * left + taps[1] * middle + taps[2] * right + shift

    return jax.vmap(one)(ext, dilation, w_time.T, b_time).astype(jnp.bfloat16)


def bin_filter(padded, w_freq, b_freq, bins):
    channels = w_freq.shape[1]
    group_size = w_freq.shape[2]
    tiled = jnp.tile(w_freq, (1, 1, channels // group_size))
    owner = jnp.arange(channels) // group_size
    keep = owner[:, None] == owner[None, :]
    blocks = jnp.where(keep[None], tiled, jnp.zeros_like(tiled))
    total = jnp.einsum(
        "co,cft->oft", blocks[0], padded[:, 0:bins], preferred_element_type=jnp.float32
    )
    for tap in range(1, w_freq.shape[0]):
        total = total + jnp.einsum(
            "co,cft->oft",
            blocks[tap],
            padded[:, tap : tap + bins],
            preferred_element_type=jnp.float32,
        )
    return jax.nn.gelu(total + b_freq[:, None, None], approximate=True).astype(jnp.bfloat16)


def on_device(
    spectrum,
    w_freq,
    b_freq,
    dilation,
    w_time,
    b_time,
    w_mix,
    ln_gain,
    w_up,
    b_up,
    w_down,
    b_down,
    epoch_lengths,
):
    channels = spectrum.shape[0]
    local_bins = spectrum.shape[1]
    block_frames = spectrum.shape[2]
    bands = lax.axis_size("band")
    piece = block_frames // bands
    all_bins = local_bins * bands
    padded = padded_2(spectrum, (("band", 1),), 2, False)
    spectral = bin_filter(padded, w_freq, b_freq, local_bins)
    swapped = lax.all_to_all(spectral, "band", split_axis=2, concat_axis=1, tiled=True)
    beside_all = padded_2(swapped, (("band", 2),), piece, True)
    outer_parts = jnp.concatenate([beside_all[:, :, 2 * piece :], beside_all[:, :, :piece]], axis=2)
    outer = padded_2(outer_parts, (("tm", 2),), piece, False)
    band_index = lax.axis_index("band")
    left = jnp.where(band_index == 0, outer[:, :, :piece], beside_all[:, :, :piece])
    right = jnp.where(
        band_index == bands - 1, outer[:, :, 3 * piece :], beside_all[:, :, 2 * piece :]
    )
    joined = jnp.concatenate([left, swapped, right], axis=2)
    filtered = dilated(joined, dilation, w_time, b_time, piece, piece)
    row = epoch_lengths[0]
    ends = jnp.cumsum(row)
    starts = ends - row
    frame_ids = lax.axis_index("band") * piece + jnp.arange(piece, dtype=jnp.int32)
    member = (
        (frame_ids[None, :] >= starts[:, None]) & (frame_ids[None, :] < ends[:, None])
    ).astype(jnp.float32)
    epochs_here = row.shape[0]
    bin_block = min(32, all_bins)

    def per_block(block_id):
        rows = lax.dynamic_slice_in_dim(w_mix, block_id * bin_block, bin_block, 0)
        mixed = jnp.einsum("gf,cfp->cgp", rows, filtered, preferred_element_type=jnp.float32)
        mean = jnp.mean(mixed, axis=0)
        var = jnp.mean((mixed - mean) ** 2, axis=0)
        normed = ((mixed - mean) * lax.rsqrt(var + 1e-05) * ln_gain[:, None, None]).astype(
            jnp.bfloat16
        )
        flat = normed.reshape(channels, bin_block * piece)
        hidden = (
            jnp.einsum("ch,cn->hn", w_up, flat, preferred_element_type=jnp.float32) + b_up[:, None]
        )
        hidden = jax.nn.gelu(hidden, approximate=True).astype(jnp.bfloat16)
        projected = (
            jnp.einsum("hc,hn->cn", w_down, hidden, preferred_element_type=jnp.float32)
            + b_down[:, None]
        )
        resid = lax.dynamic_slice_in_dim(filtered, block_id * bin_block, bin_block, 1).astype(
            jnp.float32
        )
        block_out = projected.reshape(channels, bin_block, piece) + resid
        sums = jnp.einsum("et,cft->efc", member, block_out, precision=lax.Precision.HIGHEST)
        squares = jnp.einsum(
            "et,cft->efc", member, block_out * block_out, precision=lax.Precision.HIGHEST
        )
        return (sums, squares)

    sums, squares = lax.map(per_block, jnp.arange(all_bins // bin_block, dtype=jnp.int32))
    sums = jnp.transpose(sums, (1, 0, 2, 3)).reshape(epochs_here, all_bins * channels)
    squares = jnp.transpose(squares, (1, 0, 2, 3)).reshape(epochs_here, all_bins * channels)
    total_sums, total_squares = (
        lax.psum_scatter(sums, "band", scatter_dimension=1, tiled=True),
        lax.psum_scatter(squares, "band", scatter_dimension=1, tiled=True),
    )
    lens = row.astype(jnp.float32)[:, None]
    return (total_sums / lens, total_squares / lens)


def solution(mesh):
    return jax.shard_map(
        on_device,
        mesh=mesh,
        in_specs=(
            P(None, "band", "tm"),
            P(),
            P(),
            P(),
            P(),
            P(),
            P(),
            P(),
            P(),
            P(),
            P(),
            P(),
            P("tm", None),
        ),
        out_specs=(P("tm", "band"), P("tm", "band")),
        check_vma=False,
    )
```

profile of v0, /device:TPU:1, one launch (start us, length us, event | category | flops | bytes accessed | tf_op | source)
XLA Modules:
  0.0 469.6 jit_solution(17832737130556438430)
XLA Ops:
  7.2 3.3 fusion.61
  10.7 4.5 collective-permute-start
  15.4 5.6 %collective-permute-start.1 = (bf16[64,2,2048]{2,0,1:T(8,128)(2,1)S(1)}, bf16[64,2,2048]{2,0,1:T(8,128)(2,1)S(1)}, u32[]{:S(2)}, u32[]{:S(2)}) collective-permute-start(bf16[64,2,2048]{2,0,1:T(8,128)(2,1)S(1)} %copy.78), channel_id=1, source_target_pairs={{32,0},{64,32},{96,64},{128,96},{160,128},{192,160},{224,192},{256... | collective-permute-start | bytes 1572872 | tf_op jit(solution)/shard_map/ppermute | solution.py:17
  21.1 2.8 fusion.54
  23.9 1.2 constant_dynamic-update-slice_fusion
  27.3 2.6 fusion.43
  30.0 4.3 copy.55
  34.2 6.3 %reshape.163 = bf16[16,2,32768]{2,1,0:T(2,128)(2,1)S(1)} reshape(bf16[2048,8,64]{2,1,0:T(8,128)(2,1)} %bitcast.139) | data formatting | bytes 4194304
  40.6 36.4 %all_to_all.18 = bf16[16,2,32768]{2,1,0:T(2,128)(2,1)} all-to-all(bf16[16,2,32768]{2,1,0:T(2,128)(2,1)S(1)} %reshape.163), channel_id=1, replica_groups=mesh['band'=16,'tm'=32] {'band'}, dimensions={0} | all-to-all | bytes 4194304 | tf_op jit(solution)/shard_map/all_to_all | solution.py:76
  77.0 7.4 %reshape.164 = bf16[2048,8,64]{2,1,0:T(8,128)(2,1)} reshape(bf16[16,2,32768]{2,1,0:T(2,128)(2,1)} %all_to_all.18) | data formatting | bytes 4194304
  84.4 6.9 %copy.57 = bf16[64,16,8,128]{3,2,1,0:T(8,128)(2,1)} copy(bf16[64,16,8,128]{0,2,3,1:T(8,128)(2,1)} %bitcast.140) | data formatting | bytes 4194304 | tf_op jit(solution)/shard_map/all_to_all | solution.py:76
  91.3 3.3 copy.58
  94.6 1.9 collective-permute-start.2
  96.6 3.3 collective-permute-start.4
  99.9 19.6 %collective-permute-done.2 = bf16[64,128,128]{1,0,2:T(8,128)(2,1)} collective-permute-done((bf16[64,128,128]{1,0,2:T(8,128)(2,1)S(1)}, bf16[64,128,128]{1,0,2:T(8,128)(2,1)}, u32[]{:S(2)}, u32[]{:S(2)}) %collective-permute-start.2) | collective-permute-done | bytes 2097184 | tf_op jit(solution)/shard_map/ppermute | solution.py:14
  119.5 5.1 %collective-permute-start.3 = (bf16[64,128,128]{1,0,2:T(8,128)(2,1)}, bf16[64,128,128]{1,0,2:T(8,128)(2,1)}, u32[]{:S(2)}, u32[]{:S(2)}) collective-permute-start(bf16[64,128,128]{1,0,2:T(8,128)(2,1)} %collective-permute-done.2), channel_id=1, source_target_pairs={{0,1},{1,2},{2,3},{3,4},{4,5},{5,6},{6,7},{7,8},{8,9},{9,10},{10,1... | collective-permute-start | bytes 6291464 | tf_op jit(solution)/shard_map/ppermute | solution.py:14
  124.6 1.3 collective-permute-start.5
  126.2 34.7 %collective-permute-done.3 = bf16[64,128,128]{1,0,2:T(8,128)(2,1)} collective-permute-done((bf16[64,128,128]{1,0,2:T(8,128)(2,1)}, bf16[64,128,128]{1,0,2:T(8,128)(2,1)}, u32[]{:S(2)}, u32[]{:S(2)}) %collective-permute-start.3) | collective-permute-done | bytes 2097184 | tf_op jit(solution)/shard_map/ppermute | solution.py:14
  160.9 1.8 broadcast_select_fusion.1
  162.7 3.4 collective-permute-done.5
  166.1 1.8 broadcast_select_fusion
  167.9 5.7 %pad_maximum_fusion = bf16[64,128,384]{1,0,2:T(8,128)(2,1)} fusion(bf16[64,128,128]{1,0,2:T(8,128)(2,1)S(1)} %broadcast_select_fusion, bf16[64,128,128]{1,0,2:T(8,128)(2,1)S(1)} %copy.58, bf16[64,128,128]{1,0,2:T(8,128)(2,1)S(1)} %broadcast_select_fusion.1), kind=kLoop, calls=%fused_computation.47 | loop fusion | flops 6291456 | bytes 12582912 | tf_op jit(solution)/shard_map/concatenate | solution.py:85
  173.6 9.8 %gather_fusion = bf16[64,128,128]{1,0,2:T(8,128)(2,1)} fusion(bf16[64,128,384]{1,0,2:T(8,128)(2,1)} %pad_maximum_fusion, s32[64]{0:T(128)S(1)} %get-tuple-element.195), kind=kCustom, calls=%fused_computation | custom fusion | bytes 4195072 | tf_op jit(solution)/shard_map/vmap()/gather | solution.py:25
  183.4 9.8 %gather_fusion.1 = bf16[64,128,128]{1,0,2:T(8,128)(2,1)} fusion(bf16[64,128,384]{1,0,2:T(8,128)(2,1)} %pad_maximum_fusion, s32[64]{0:T(128)S(1)} %get-tuple-element.196), kind=kCustom, calls=%fused_computation.1 | custom fusion | bytes 4195072 | tf_op jit(solution)/shard_map/vmap()/gather | solution.py:27
  193.2 5.2 %add_convert_fusion = bf16[64,128,128]{1,0,2:T(8,128)(2,1)} fusion(bf16[64,128,128]{1,0,2:T(8,128)(2,1)} %gather_fusion.1, bf16[64,128,128]{1,0,2:T(8,128)(2,1)S(1)} %copy.58, bf16[64,128,128]{1,0,2:T(8,128)(2,1)} %gather_fusion, f32[64]{0:T(128)S(1)} %copy-done.5, f32[64]{0:T(128)S(1)} %get-tuple-element.191, f32[64]{0:T(128)S(1)} %get-tuple-element.192, ...), kind=kLoop, calls=%fused_computation.57 | loop fusion | flops 10485760 | bytes 8389632 | tf_op jit(solution)/shard_map/convert_element_type | solution.py:30
  198.4 3.4 copy.62
  201.8 67.5 %while.13 = (s32[]{:T(128)}, f32[4,8,32,64]{2,1,3,0:T(8,128)}, f32[4,8,32,64]{2,1,3,0:T(8,128)}, s32[4]{0:T(128)S(1)}, bf16[128,128]{1,0:T(8,128)(2,1)}, /*index...) while((s32[]{:T(128)}, f32[4,8,32,64]{2,1,3,0:T(8,128)}, ...), condition=%wide.region_4.5_spmd.clone, body=%wide.region_1.4_spmd.clone.sunk | while | flops 399519744 | bytes 14905191 | solution.py:124
  203.3 1.1 fusion.86
  205.6 3.1 fusion.87
  209.1 4.9 %fusion.89 = f32[4,8,32,64]{2,1,3,0:T(8,128)} fusion(f32[4,8,32,64]{2,1,3,0:T(8,128)} %get-tuple-element.306, s32[]{:T(128)} %get-tuple-element.304, f32[64,32,128]{2,1,0:T(8,128)S(1)} %bitcast_add_fusion.2, s32[128]{0:T(128)S(1)} %get-tuple-element.335, s32[8]{0:T(128)S(1)} %get-tuple-element.334, s32[8]{0:T(128)S(1)} %get-tuple-element.333), kind=kOutput, calls=%fused_computation.18.clone.1 | convolution fusion | flops 25432064 | bytes 1311808 | tf_op jit(solution)/shard_map/while/body/eval_jaxpr/et,cft->efc/dot_general | solution.py:119
  214.0 4.9 %fusion.88 = f32[4,8,32,64]{2,1,3,0:T(8,128)} fusion(f32[4,8,32,64]{2,1,3,0:T(8,128)} %get-tuple-element.305, s32[]{:T(128)} %get-tuple-element.304, f32[64,32,128]{2,1,0:T(8,128)S(1)} %bitcast_add_fusion.2, s32[128]{0:T(128)S(1)} %get-tuple-element.335, s32[8]{0:T(128)S(1)} %get-tuple-element.334, s32[8]{0:T(128)S(1)} %get-tuple-element.333), kind=kOutput, calls=%fused_computation.20.clone.1 | convolution fusion | flops 25169920 | bytes 1311808 | tf_op jit(solution)/shard_map/while/body/eval_jaxpr/et,cft->efc/dot_general | solution.py:118
  220.1 1.1 fusion.86
  222.4 3.1 fusion.87
  225.9 4.9 %fusion.89 = f32[4,8,32,64]{2,1,3,0:T(8,128)} fusion(f32[4,8,32,64]{2,1,3,0:T(8,128)} %get-tuple-element.306, s32[]{:T(128)} %get-tuple-element.304, f32[64,32,128]{2,1,0:T(8,128)S(1)} %bitcast_add_fusion.2, s32[128]{0:T(128)S(1)} %get-tuple-element.335, s32[8]{0:T(128)S(1)} %get-tuple-element.334, s32[8]{0:T(128)S(1)} %get-tuple-element.333), kind=kOutput, calls=%fused_computation.18.clone.1 | convolution fusion | flops 25432064 | bytes 1311808 | tf_op jit(solution)/shard_map/while/body/eval_jaxpr/et,cft->efc/dot_general | solution.py:119
  230.8 4.9 %fusion.88 = f32[4,8,32,64]{2,1,3,0:T(8,128)} fusion(f32[4,8,32,64]{2,1,3,0:T(8,128)} %get-tuple-element.305, s32[]{:T(128)} %get-tuple-element.304, f32[64,32,128]{2,1,0:T(8,128)S(1)} %bitcast_add_fusion.2, s32[128]{0:T(128)S(1)} %get-tuple-element.335, s32[8]{0:T(128)S(1)} %get-tuple-element.334, s32[8]{0:T(128)S(1)} %get-tuple-element.333), kind=kOutput, calls=%fused_computation.20.clone.1 | convolution fusion | flops 25169920 | bytes 1311808 | tf_op jit(solution)/shard_map/while/body/eval_jaxpr/et,cft->efc/dot_general | solution.py:118
  236.9 1.1 fusion.86
  239.2 3.1 fusion.87
  242.7 4.9 %fusion.89 = f32[4,8,32,64]{2,1,3,0:T(8,128)} fusion(f32[4,8,32,64]{2,1,3,0:T(8,128)} %get-tuple-element.306, s32[]{:T(128)} %get-tuple-element.304, f32[64,32,128]{2,1,0:T(8,128)S(1)} %bitcast_add_fusion.2, s32[128]{0:T(128)S(1)} %get-tuple-element.335, s32[8]{0:T(128)S(1)} %get-tuple-element.334, s32[8]{0:T(128)S(1)} %get-tuple-element.333), kind=kOutput, calls=%fused_computation.18.clone.1 | convolution fusion | flops 25432064 | bytes 1311808 | tf_op jit(solution)/shard_map/while/body/eval_jaxpr/et,cft->efc/dot_general | solution.py:119
  247.6 4.9 %fusion.88 = f32[4,8,32,64]{2,1,3,0:T(8,128)} fusion(f32[4,8,32,64]{2,1,3,0:T(8,128)} %get-tuple-element.305, s32[]{:T(128)} %get-tuple-element.304, f32[64,32,128]{2,1,0:T(8,128)S(1)} %bitcast_add_fusion.2, s32[128]{0:T(128)S(1)} %get-tuple-element.335, s32[8]{0:T(128)S(1)} %get-tuple-element.334, s32[8]{0:T(128)S(1)} %get-tuple-element.333), kind=kOutput, calls=%fused_computation.20.clone.1 | convolution fusion | flops 25169920 | bytes 1311808 | tf_op jit(solution)/shard_map/while/body/eval_jaxpr/et,cft->efc/dot_general | solution.py:118
  253.7 1.1 fusion.86
  256.0 3.1 fusion.87
  259.5 4.9 %fusion.89 = f32[4,8,32,64]{2,1,3,0:T(8,128)} fusion(f32[4,8,32,64]{2,1,3,0:T(8,128)} %get-tuple-element.306, s32[]{:T(128)} %get-tuple-element.304, f32[64,32,128]{2,1,0:T(8,128)S(1)} %bitcast_add_fusion.2, s32[128]{0:T(128)S(1)} %get-tuple-element.335, s32[8]{0:T(128)S(1)} %get-tuple-element.334, s32[8]{0:T(128)S(1)} %get-tuple-element.333), kind=kOutput, calls=%fused_computation.18.clone.1 | convolution fusion | flops 25432064 | bytes 1311808 | tf_op jit(solution)/shard_map/while/body/eval_jaxpr/et,cft->efc/dot_general | solution.py:119
  264.4 4.9 %fusion.88 = f32[4,8,32,64]{2,1,3,0:T(8,128)} fusion(f32[4,8,32,64]{2,1,3,0:T(8,128)} %get-tuple-element.305, s32[]{:T(128)} %get-tuple-element.304, f32[64,32,128]{2,1,0:T(8,128)S(1)} %bitcast_add_fusion.2, s32[128]{0:T(128)S(1)} %get-tuple-element.335, s32[8]{0:T(128)S(1)} %get-tuple-element.334, s32[8]{0:T(128)S(1)} %get-tuple-element.333), kind=kOutput, calls=%fused_computation.20.clone.1 | convolution fusion | flops 25169920 | bytes 1311808 | tf_op jit(solution)/shard_map/while/body/eval_jaxpr/et,cft->efc/dot_general | solution.py:118
  269.3 1.5 copy.63
  271.8 1.5 copy.64
  274.3 94.7 %reduce-scatter.3.cloned.1.call-done = f32[8,512]{1,0:T(8,128)} async-done(((f32[8,8192]{1,0:T(8,128)}), f32[8,512]{1,0:T(8,128)}) %reduce-scatter.3.cloned.1.call-update) | async-done | bytes 16400 | tf_op jit(solution)/shard_map/reduce_scatter | solution.py:128
  369.0 92.3 %reduce-scatter.5.cloned.1.call-done = f32[8,512]{1,0:T(8,128)} async-done(((f32[8,8192]{1,0:T(8,128)}), f32[8,512]{1,0:T(8,128)}) %reduce-scatter.5.cloned.1.call-update) | async-done | bytes 16400 | tf_op jit(solution)/shard_map/reduce_scatter | solution.py:129
  461.3 1.4 broadcast_divide_fusion
  (80 shorter events, 13.1 us)
Async XLA Ops:
  7.2 13.9 %copy-start = (bf16[64,8,2048]{2,1,0:T(8,128)(2,1)S(1)}, bf16[64,8,2048]{2,1,0:T(8,128)(2,1)}, u32[]{:S(2)}) copy-start(bf16[64,8,2048]{2,1,0:T(8,128)(2,1)} %param.15) | copy-start | bytes 6291460
  7.2 13.9 %copy-start.2 = (bf16[5,64,8]{1,2,0:T(8,128)(2,1)S(1)}, bf16[5,64,8]{1,2,0:T(8,128)(2,1)}, u32[]{:S(2)}) copy-start(bf16[5,64,8]{1,2,0:T(8,128)(2,1)} %param.16) | copy-start | bytes 15364
  7.2 361.8 %reduce-scatter.3.cloned.1.call-start = ((), (), s32[]{:S(2)}) async-start(), calls=%async_computation.3 | async-start | bytes 278528 | tf_op jit(solution)/shard_map/reduce_scatter | solution.py:128
  10.7 13.2 %collective-permute-start = (bf16[64,2,2048]{2,0,1:T(8,128)(2,1)S(1)}, bf16[64,2,2048]{2,0,1:T(8,128)(2,1)S(1)}, u32[]{:S(2)}, u32[]{:S(2)}) collective-permute-start(bf16[64,2,2048]{2,0,1:T(8,128)(2,1)S(1)} %copy.79), channel_id=1, source_target_pairs={{0,32},{32,64},{64,96},{96,128},{128,160},{160,192},{192,224},{224... | collective-permute-start | bytes 1572872 | tf_op jit(solution)/shard_map/ppermute | solution.py:14
  15.4 11.2 %collective-permute-start.1 = (bf16[64,2,2048]{2,0,1:T(8,128)(2,1)S(1)}, bf16[64,2,2048]{2,0,1:T(8,128)(2,1)S(1)}, u32[]{:S(2)}, u32[]{:S(2)}) collective-permute-start(bf16[64,2,2048]{2,0,1:T(8,128)(2,1)S(1)} %copy.78), channel_id=1, source_target_pairs={{32,0},{64,32},{96,64},{128,96},{160,128},{192,160},{224,192},{256... | collective-permute-start | bytes 1572872 | tf_op jit(solution)/shard_map/ppermute | solution.py:17
  26.6 0.7 copy-start.4
  91.3 34.6 %copy-start.11 = (s32[1,8]{1,0:T(1,128)S(1)}, s32[1,8]{1,0:T(1,128)}, u32[]{:S(2)}) copy-start(s32[1,8]{1,0:T(1,128)} %param.27) | copy-start | bytes 100
  91.3 34.8 %copy-start.9 = (s32[64]{0:T(128)S(1)}, s32[64]{0:T(128)}, u32[]{:S(2)}) copy-start(s32[64]{0:T(128)} %param.18) | copy-start | bytes 772
  91.3 34.8 %copy-start.3 = (f32[3,64]{1,0:T(4,128)S(1)}, f32[3,64]{1,0:T(4,128)}, u32[]{:S(2)}) copy-start(f32[3,64]{1,0:T(4,128)} %param.19) | copy-start | bytes 2308
  94.6 24.9 %collective-permute-start.2 = (bf16[64,128,128]{1,0,2:T(8,128)(2,1)S(1)}, bf16[64,128,128]{1,0,2:T(8,128)(2,1)}, u32[]{:S(2)}, u32[]{:S(2)}) collective-permute-start(bf16[64,128,128]{1,0,2:T(8,128)(2,1)S(1)} %copy.58), channel_id=1, source_target_pairs={{0,32},{32,64},{64,96},{96,128},{128,160},{160,192},{192,224},{224... | collective-permute-start | bytes 6291464 | tf_op jit(solution)/shard_map/ppermute | solution.py:14
  96.6 28.0 %collective-permute-start.4 = (bf16[64,128,128]{1,0,2:T(8,128)(2,1)S(1)}, bf16[64,128,128]{1,0,2:T(8,128)(2,1)}, u32[]{:S(2)}, u32[]{:S(2)}) collective-permute-start(bf16[64,128,128]{1,0,2:T(8,128)(2,1)S(1)} %copy.58), channel_id=1, source_target_pairs={{32,0},{64,32},{96,64},{128,96},{160,128},{192,160},{224,192},{256... | collective-permute-start | bytes 6291464 | tf_op jit(solution)/shard_map/ppermute | solution.py:17
  119.5 41.4 %collective-permute-start.3 = (bf16[64,128,128]{1,0,2:T(8,128)(2,1)}, bf16[64,128,128]{1,0,2:T(8,128)(2,1)}, u32[]{:S(2)}, u32[]{:S(2)}) collective-permute-start(bf16[64,128,128]{1,0,2:T(8,128)(2,1)} %collective-permute-done.2), channel_id=1, source_target_pairs={{0,1},{1,2},{2,3},{3,4},{4,5},{5,6},{6,7},{7,8},{8,9},{9,10},{10,1... | collective-permute-start | bytes 6291464 | tf_op jit(solution)/shard_map/ppermute | solution.py:14
  124.6 41.5 %collective-permute-start.5 = (bf16[64,128,128]{1,0,2:T(8,128)(2,1)}, bf16[64,128,128]{1,0,2:T(8,128)(2,1)}, u32[]{:S(2)}, u32[]{:S(2)}) collective-permute-start(bf16[64,128,128]{1,0,2:T(8,128)(2,1)} %collective-permute-done.4), channel_id=1, source_target_pairs={{1,0},{2,1},{3,2},{4,3},{5,4},{6,5},{7,6},{8,7},{9,8},{10,9},{11,1... | collective-permute-start | bytes 6291464 | tf_op jit(solution)/shard_map/ppermute | solution.py:17
  183.4 9.8 %copy-start.5 = (f32[64]{0:T(128)S(1)}, f32[64]{0:T(128)}, u32[]{:S(2)}) copy-start(f32[64]{0:T(128)} %param.20) | copy-start | bytes 772
  198.4 3.4 copy-start.1
  198.4 3.4 copy-start.6
  198.4 3.4 copy-start.7
  198.4 3.4 copy-start.8
  198.4 3.4 copy-start.10
  271.8 189.6 %reduce-scatter.5.cloned.1.call-start = ((), (), s32[]{:S(2)}) async-start(), calls=%async_computation.4 | async-start | bytes 278528 | tf_op jit(solution)/shard_map/reduce_scatter | solution.py:129
Sparse Core Ops, SparseCore 0:
  271.9 97.0 reduce-scatter.2
  373.6 87.6 reduce-scatter.4
where the time goes:
time: 472 us; the launch traced here: 470 us
  waiting for transfers between devices  245 us (52%)
  local copies, waits for them, and re-layouts  64.1 us (14%)
  matrix products  63.5 us (13%)
  blocking collectives  36.4 us (8%)
  starting transfers between devices  21.8 us (5%)
  other arithmetic  21.6 us (5%)
  between operations  14.4 us (3%)
    reduce_scatter x1, waiting for transfers between devices, on_device(): lax.psum_scatter(sums, 'band', scatter_dimension=1, tiled=True)  94.7 us
    reduce_scatter x1, waiting for transfers between devices, on_device(): lax.psum_scatter(squares, 'band', scatter_dimension=1, tiled=True)  92.3 us
    ppermute x3, waiting for transfers between devices, padded_2(): lax.ppermute(lax.slice_in_dim(block, block.shape[dim] - width, None, axis...  54.3 us
    all_to_all x1, blocking collectives, on_device(): lax.all_to_all(spectral, 'band', split_axis=2, concat_axis=1, tiled=True)  36.4 us
    dot_general x4, matrix products, per_block(): jnp.einsum('et,cft->efc', member, block_out, precision=lax.Precision.HIGH...  19.6 us
    dot_general x4, matrix products, per_block(): jnp.einsum('et,cft->efc', member, block_out * block_out, precision=lax.Pr...  19.6 us
    unnamed x30, local copies, waits for them, and re-layouts  17.5 us
    dot_general x4, matrix products, per_block(): jnp.einsum('hc,hn->cn', w_down, hidden, preferred_element_type=jnp.float32)  12.4 us
  transfers between devices with their start and end apart: 8, of which 5 were waited for; matrix products, arithmetic and copies ran while one was open for 2% of the time, Pallas kernels for 0%

commit v1 on v0

--- a/solution.py
+++ b/solution.py
@@ -71,19 +71,18 @@
     bands = lax.axis_size("band")
     piece = block_frames // bands
     all_bins = local_bins * bands
-    padded = padded_2(spectrum, (("band", 1),), 2, False)
+    reach = 128
+    longer = padded_2(spectrum, (("tm", 2),), reach, False)
+    padded = padded_2(longer, (("band", 1),), 2, False)
     spectral = bin_filter(padded, w_freq, b_freq, local_bins)
-    swapped = lax.all_to_all(spectral, "band", split_axis=2, concat_axis=1, tiled=True)
-    beside_all = padded_2(swapped, (("band", 2),), piece, True)
-    outer_parts = jnp.concatenate([beside_all[:, :, 2 * piece :], beside_all[:, :, :piece]], axis=2)
-    outer = padded_2(outer_parts, (("tm", 2),), piece, False)
-    band_index = lax.axis_index("band")
-    left = jnp.where(band_index == 0, outer[:, :, :piece], beside_all[:, :, :piece])
-    right = jnp.where(
-        band_index == bands - 1, outer[:, :, 3 * piece :], beside_all[:, :, 2 * piece :]
-    )
-    joined = jnp.concatenate([left, swapped, right], axis=2)
-    filtered = dilated(joined, dilation, w_time, b_time, piece, piece)
+    tm = lax.axis_index("tm")
+    frame = tm * block_frames - reach + jnp.arange(block_frames + 2 * reach, dtype=jnp.int32)
+    inside = (frame >= 0) & (frame < lax.axis_size("tm") * block_frames)
+    spectral = jnp.where(inside, spectral, jnp.zeros_like(spectral))
+    filtered = dilated(spectral, dilation, w_time, b_time, reach, block_frames)
+    parts = jnp.transpose(filtered.reshape(channels, local_bins, bands, piece), (2, 0, 1, 3))
+    swapped = lax.all_to_all(parts, "band", split_axis=0, concat_axis=0, tiled=True)
+    filtered = jnp.transpose(swapped, (1, 0, 2, 3)).reshape(channels, all_bins, piece)
     row = epoch_lengths[0]
     ends = jnp.cumsum(row)
     starts = ends - row
@@ -124,10 +123,11 @@
     sums, squares = lax.map(per_block, jnp.arange(all_bins // bin_block, dtype=jnp.int32))
     sums = jnp.transpose(sums, (1, 0, 2, 3)).reshape(epochs_here, all_bins * channels)
     squares = jnp.transpose(squares, (1, 0, 2, 3)).reshape(epochs_here, all_bins * channels)
-    total_sums, total_squares = (
-        lax.psum_scatter(sums, "band", scatter_dimension=1, tiled=True),
-        lax.psum_scatter(squares, "band", scatter_dimension=1, tiled=True),
+    both = jnp.stack([sums, squares]).reshape(2, epochs_here, bands, local_bins * channels)
+    both = lax.all_to_all(
+        jnp.transpose(both, (2, 0, 1, 3)), "band", split_axis=0, concat_axis=0, tiled=True
     )
+    total_sums, total_squares = jnp.sum(both, axis=0)
     lens = row.astype(jnp.float32)[:, None]
     return (total_sums / lens, total_squares / lens)
 

time: 472 us -> 621 us (1.32)
  the two profiles are of different devices: /device:TPU:1 before, /device:TPU:8 now
where the time goes in v1:
time: 621 us; the launch traced here: 609 us
  local copies, waits for them, and re-layouts  446 us (72%)
  matrix products  62.2 us (10%)
  waiting for transfers between devices  41.2 us (7%)
  starting transfers between devices  38.6 us (6%)
  other arithmetic  17.2 us (3%)
    gather x384, local copies, waits for them, and re-layouts  424 us
    all_to_all x1, waiting for transfers between devices, on_device(): lax.all_to_all(parts, 'band', split_axis=0, concat_axis=0, tiled=True)  28.9 us
    dot_general x4, matrix products, per_block(): jnp.einsum('et,cft->efc', member, block_out * block_out, precision=lax.Pr...  19.6 us
    dot_general x4, matrix products, per_block(): jnp.einsum('et,cft->efc', member, block_out, precision=lax.Precision.HIGH...  19.6 us
    all_to_all x1, starting transfers between devices, on_device(): lax.all_to_all(parts, 'band', split_axis=0, concat_axis=0, tiled=True)  16.5 us
    unnamed x29, local copies, waits for them, and re-layouts  13.1 us
    dot_general x4, matrix products, per_block(): jnp.einsum('hc,hn->cn', w_down, hidden, preferred_element_type=jnp.float32)  12.4 us
  transfers between devices with their start and end apart: 6, of which 2 were waited for; matrix products, arithmetic and copies ran while one was open for 1% of the time, Pallas kernels for 0%

profile of v1, /device:TPU:8, one launch (start us, length us, event | category | flops | bytes accessed | tf_op | source)
XLA Modules:
  0.0 609.1 jit_solution(8705647268733191771)
XLA Ops:
  1.7 3.8 collective-permute-start
  5.5 9.4 %collective-permute-start.1 = (bf16[64,8,128]{2,0,1:T(8,128)(2,1)S(1)}, bf16[64,8,128]{2,0,1:T(8,128)(2,1)S(1)}, u32[]{:S(2)}, u32[]{:S(2)}) collective-permute-start(bf16[64,8,128]{2,0,1:T(8,128)(2,1)S(1)} %copy.58), channel_id=1, source_target_pairs={{1,0},{2,1},{3,2},{4,3},{5,4},{6,5},{7,6},{8,7},{9,8},{10,9},{11,1... | collective-permute-start | bytes 393224 | tf_op jit(solution)/shard_map/ppermute | solution.py:17
  16.5 2.7 constant_dynamic-update-slice_fusion.1
  20.7 3.1 collective-permute-start.2
  26.8 3.1 fusion.48
  34.3 210.7 %while.15 = (s32[]{:T(128)}, bf16[64,8,2304]{2,1,0:T(8,128)(2,1)}, s32[64,3]{0,1:T(4,128)S(1)}, bf16[64,8,2048]{2,1,0:T(8,128)(2,1)}, s32[]{:T(128)}) while((s32[]{:T(128)}, bf16[64,8,2304]{2,1,0:T(8,128)(2,1)}, s32[64,3]{0,1:T(4,128)S(1)}, bf16[64,8,2048]{2,1,0:T(8,128)(2,1)}, s32[]{:T(128)}) %tuple.73), condition=%wide.while_cond, body=%wide.while_body.sunk | while | flops 2 | bytes 67177 | solution.py:25
  246.5 213.6 %while.16 = (s32[]{:T(128)}, bf16[64,8,2304]{2,1,0:T(8,128)(2,1)}, s32[64,3]{0,1:T(4,128)S(1)}, bf16[64,8,2048]{2,1,0:T(8,128)(2,1)}, s32[]{:T(128)}) while((s32[]{:T(128)}, bf16[64,8,2304]{2,1,0:T(8,128)(2,1)}, s32[64,3]{0,1:T(4,128)S(1)}, bf16[64,8,2048]{2,1,0:T(8,128)(2,1)}, s32[]{:T(128)}) %tuple.79), condition=%wide.while_cond.1, body=%wide.while_body.1.sunk | while | flops 2 | bytes 67177 | solution.py:27
  263.8 2.7 dynamic-slice_dynamic-update-slice_fusion.5
  267.2 2.7 dynamic-slice_dynamic-update-slice_fusion.5
  273.8 2.7 dynamic-slice_dynamic-update-slice_fusion.5
  283.8 2.7 dynamic-slice_dynamic-update-slice_fusion.5
  287.2 2.7 dynamic-slice_dynamic-update-slice_fusion.5
  300.5 2.7 dynamic-slice_dynamic-update-slice_fusion.5
  327.2 2.7 dynamic-slice_dynamic-update-slice_fusion.5
  330.6 2.7 dynamic-slice_dynamic-update-slice_fusion.5
  333.9 2.8 dynamic-slice_dynamic-update-slice_fusion.5
  337.3 2.7 dynamic-slice_dynamic-update-slice_fusion.5
  340.6 2.7 dynamic-slice_dynamic-update-slice_fusion.5
  344.0 2.7 dynamic-slice_dynamic-update-slice_fusion.5
  350.6 2.7 dynamic-slice_dynamic-update-slice_fusion.5
  360.7 2.7 dynamic-slice_dynamic-update-slice_fusion.5
  364.0 2.7 dynamic-slice_dynamic-update-slice_fusion.5
  380.7 2.7 dynamic-slice_dynamic-update-slice_fusion.5
  384.0 2.7 dynamic-slice_dynamic-update-slice_fusion.5
  394.1 2.7 dynamic-slice_dynamic-update-slice_fusion.5
  397.4 2.7 dynamic-slice_dynamic-update-slice_fusion.5
  414.1 2.7 dynamic-slice_dynamic-update-slice_fusion.5
  417.4 2.7 dynamic-slice_dynamic-update-slice_fusion.5
  450.8 2.7 dynamic-slice_dynamic-update-slice_fusion.5
  460.2 9.4 %bitcast_bitcast_fusion = bf16[16,64,8,128]{3,1,2,0:T(8,128)(2,1)} fusion(bf16[64,8,2304]{2,0,1:T(8,128)(2,1)S(1)} %fusion.48, bf16[64,8,2048]{2,1,0:T(8,128)(2,1)} %get-tuple-element.82, bf16[64,8,2048]{2,1,0:T(8,128)(2,1)} %get-tuple-element.74, f32[64]{0:T(128)S(1)} %copy-done.4, f32[64]{0:T(128)S(1)} %get-tuple-element.211, ...), kind=kLoop, calls=%fused_computation.79 | loop fusion | flops 10485760 | bytes 8390656 | tf_op jit(solution)/shard_map/transpose | solution.py:83
  469.6 16.5 %all-to-all-start = ((bf16[16,64,8,128]{3,1,2,0:T(8,128)(2,1)}), bf16[16,64,8,128]{3,1,2,0:T(8,128)(2,1)S(1)}, u32[]{:S(2)}, u32[]{:S(2)}) async-start(bf16[16,64,8,128]{3,1,2,0:T(8,128)(2,1)} %bitcast_bitcast_fusion), calls=%async_computation | async-start | bytes 4194304 | tf_op jit(solution)/shard_map/all_to_all | solution.py:84
  486.3 28.9 %all-to-all-done = bf16[16,64,8,128]{3,1,2,0:T(8,128)(2,1)S(1)} async-done(((bf16[16,64,8,128]{3,1,2,0:T(8,128)(2,1)}), bf16[16,64,8,128]{3,1,2,0:T(8,128)(2,1)S(1)}, u32[]{:S(2)}, u32[]{:S(2)}) %all-to-all-start) | async-done | bytes 2097184 | tf_op jit(solution)/shard_map/all_to_all | solution.py:84
  516.6 2.9 copy.41
  519.6 67.3 %while.17 = (s32[]{:T(128)}, f32[4,8,32,64]{2,1,3,0:T(8,128)}, f32[4,8,32,64]{2,1,3,0:T(8,128)}, s32[4]{0:T(128)S(1)}, bf16[128,128]{1,0:T(8,128)(2,1)}, /*index...) while((s32[]{:T(128)}, f32[4,8,32,64]{2,1,3,0:T(8,128)}, ...), condition=%wide.region_4.5_spmd.clone, body=%wide.region_1.4_spmd.clone.sunk | while | flops 399519744 | bytes 14905191 | solution.py:123
  523.1 3.1 fusion.107
  526.6 4.9 fusion.109
  531.5 4.9 fusion.108
  540.0 3.1 fusion.107
  543.5 4.9 fusion.109
  548.4 4.9 fusion.108
  556.8 3.1 fusion.107
  560.3 4.9 fusion.109
  565.2 4.9 fusion.108
  573.6 3.1 fusion.107
  577.1 4.9 fusion.109
  582.0 4.9 fusion.108
  591.5 4.6 all-to-all-start.1
  596.1 12.3 %all-to-all-done.1 = f32[16,2,8,512]{3,2,1,0:T(8,128)S(1)} async-done(((f32[16,2,8,512]{3,2,1,0:T(8,128)}), f32[16,2,8,512]{3,2,1,0:T(8,128)S(1)}, u32[]{:S(2)}, u32[]{:S(2)}) %all-to-all-start.1) | async-done | bytes 524320 | tf_op jit(solution)/shard_map/all_to_all | solution.py:127
  (455 shorter events, 396.4 us)
Async XLA Ops:
  1.7 14.8 %collective-permute-start = (bf16[64,8,128]{2,0,1:T(8,128)(2,1)S(1)}, bf16[64,8,128]{2,0,1:T(8,128)(2,1)S(1)}, u32[]{:S(2)}, u32[]{:S(2)}) collective-permute-start(bf16[64,8,128]{2,0,1:T(8,128)(2,1)S(1)} %copy.57), channel_id=1, source_target_pairs={{0,1},{1,2},{2,3},{3,4},{4,5},{5,6},{6,7},{7,8},{8,9},{9,10},{10,1... | collective-permute-start | bytes 393224 | tf_op jit(solution)/shard_map/ppermute | solution.py:14
  5.5 13.7 %collective-permute-start.1 = (bf16[64,8,128]{2,0,1:T(8,128)(2,1)S(1)}, bf16[64,8,128]{2,0,1:T(8,128)(2,1)S(1)}, u32[]{:S(2)}, u32[]{:S(2)}) collective-permute-start(bf16[64,8,128]{2,0,1:T(8,128)(2,1)S(1)} %copy.58), channel_id=1, source_target_pairs={{1,0},{2,1},{3,2},{4,3},{5,4},{6,5},{7,6},{8,7},{9,8},{10,9},{11,1... | collective-permute-start | bytes 393224 | tf_op jit(solution)/shard_map/ppermute | solution.py:17
  19.2 1.5 copy-start.2
  19.4 5.2 collective-permute-start.3
  20.7 5.4 collective-permute-start.2
  26.0 0.8 copy-start.3
  32.7 427.5 %copy-start.4 = (f32[64]{0:T(128)S(1)}, f32[64]{0:T(128)}, u32[]{:S(2)}) copy-start(f32[64]{0:T(128)} %param.20) | copy-start | bytes 772
  469.6 16.6 %copy-start.9 = (s32[1,8]{1,0:T(1,128)S(1)}, s32[1,8]{1,0:T(1,128)}, u32[]{:S(2)}) copy-start(s32[1,8]{1,0:T(1,128)} %param.27) | copy-start | bytes 100
  469.6 45.7 %all-to-all-start = ((bf16[16,64,8,128]{3,1,2,0:T(8,128)(2,1)}), bf16[16,64,8,128]{3,1,2,0:T(8,128)(2,1)S(1)}, u32[]{:S(2)}, u32[]{:S(2)}) async-start(bf16[16,64,8,128]{3,1,2,0:T(8,128)(2,1)} %bitcast_bitcast_fusion), calls=%async_computation | async-start | bytes 4194304 | tf_op jit(solution)/shard_map/all_to_all | solution.py:84
  486.1 33.5 %copy-start.1 = (f32[64]{0:T(128)S(1)}, f32[64]{0:T(128)}, u32[]{:S(2)}) copy-start(f32[64]{0:T(128)} %param.22) | copy-start | bytes 772
  486.1 33.5 %copy-start.5 = (bf16[64,256]{1,0:T(8,128)(2,1)S(1)}, bf16[64,256]{1,0:T(8,128)(2,1)}, u32[]{:S(2)}) copy-start(bf16[64,256]{1,0:T(8,128)(2,1)} %param.23) | copy-start | bytes 98308
  486.1 33.5 %copy-start.6 = (bf16[256,64]{0,1:T(8,128)(2,1)S(1)}, bf16[256,64]{0,1:T(8,128)(2,1)}, u32[]{:S(2)}) copy-start(bf16[256,64]{0,1:T(8,128)(2,1)} %param.25) | copy-start | bytes 98308
  486.1 33.5 %copy-start.7 = (f32[256]{0:T(256)S(1)}, f32[256]{0:T(256)}, u32[]{:S(2)}) copy-start(f32[256]{0:T(256)} %param.24) | copy-start | bytes 3076
  486.1 33.5 %copy-start.8 = (f32[64]{0:T(128)S(1)}, f32[64]{0:T(128)}, u32[]{:S(2)}) copy-start(f32[64]{0:T(128)} %param.26) | copy-start | bytes 772
  515.2 1.3 copy-start
  591.5 16.9 %all-to-all-start.1 = ((f32[16,2,8,512]{3,2,1,0:T(8,128)}), f32[16,2,8,512]{3,2,1,0:T(8,128)S(1)}, u32[]{:S(2)}, u32[]{:S(2)}) async-start(f32[16,2,8,512]{3,2,1,0:T(8,128)} %copy.44), calls=%async_computation.1 | async-start | bytes 1048576 | tf_op jit(solution)/shard_map/all_to_all | solution.py:127

commit v2 on v1

v2 whole, which is shorter than its diff:
```python
import functools

import jax
import jax.numpy as jnp
import numpy as np
from jax import lax
from jax.experimental import pallas as pl
from jax.experimental.pallas import tpu as pltpu
from jax.sharding import PartitionSpec as P

REACH = 128
SUB = 8
GELU_C = 0.7978845608028654
GELU_A = 0.044715


def gelu(x):
    inner = x * (GELU_C + (GELU_C * GELU_A) * (x * x))
    half = 0.5 * x
    return half + half * jnp.tanh(inner)


def shifted(block, axis, step, periodic=False):
    count = lax.axis_size(axis)
    pairs = [(i, i + step) for i in range(count) if 0 <= i + step < count]
    return lax.ppermute(block, axis, pairs)


def banded_weights(w_freq, bins):
    taps, channels, size = w_freq.shape
    half = taps // 2
    place = np.zeros((taps, bins, bins + 2 * half), np.float32)
    for tap in range(taps):
        for f in range(bins):
            place[tap, f, f + tap] = 1
    grouped = w_freq.reshape(taps, channels // size, size, size)
    full = jnp.einsum(
        "kfp,kgco->gfocp",
        jnp.asarray(place, jnp.bfloat16),
        grouped,
        preferred_element_type=jnp.float32,
    ).astype(jnp.bfloat16)
    rows = bins * size
    own = full[..., half : half + bins].reshape(channels // size, rows, size * bins)
    low = full[..., :half].reshape(channels // size, rows, size * half)
    high = full[..., half + bins :].reshape(channels // size, rows, size * half)
    return jnp.concatenate([own, low, high], axis=2)


def front_kernel(bands, own_ref, low_ref, high_ref, w_ref, b_ref, taps_ref, dil_ref, flag_ref, out_ref, spec_ref):
    rows, long = own_ref.shape
    tiles = long // 128
    data = jnp.concatenate([own_ref[...], low_ref[...], high_ref[...]], axis=0)
    pre = jnp.dot(w_ref[0], data, preferred_element_type=jnp.float32)
    for j in range(tiles):
        cols = slice(j * 128, (j + 1) * 128)
        act = gelu(pre[:, cols] + b_ref[0])
        if j == 0:
            act = act * flag_ref[0, 0:1]
        if j == tiles - 1:
            act = act * flag_ref[1, 0:1]
        spec_ref[:, cols] = act.astype(jnp.bfloat16).astype(jnp.float32)
    step = dil_ref[0]
    lane = lax.broadcasted_iota(jnp.int32, (SUB, 128), 1)
    from_left = (lane - step) & 127
    from_right = (lane + step) & 127
    keep_left = lane >= step
    keep_right = lane + step < 128
    t0, t1, t2, shift = (taps_ref[0, i] for i in range(4))

    def take(value, index):
        return jnp.take_along_axis(value, index, axis=1, mode="promise_in_bounds")

    def half(start):
        v = [spec_ref[pl.ds(start, SUB), j * 128 : (j + 1) * 128] for j in range(tiles)]
        left = [take(v[j], from_left) for j in range(tiles - 1)]
        right = [take(v[j], from_right) for j in range(1, tiles)]
        outs = []
        for j in range(1, tiles - 1):
            a = jnp.where(keep_left, left[j], left[j - 1])
            c = jnp.where(keep_right, right[j - 1], right[j])
            outs.append(t0 * a + t1 * v[j] + t2 * c + shift)
        return outs

    for pair in range(rows // 16):
        top = half(pair * 16)
        bottom = half(pair * 16 + SUB)
        for j in range(bands):
            both = jnp.concatenate([top[j], bottom[j]], axis=0)
            out_ref[j, pair * 16 : (pair + 1) * 16, :] = both.astype(jnp.bfloat16)


def front(own, low, high, weights, bias, taps, dil, flags, bands):
    groups, rows, deep = weights.shape
    long = own.shape[1]
    side = low.shape[0] // groups
    return pl.pallas_call(
        functools.partial(front_kernel, bands),
        grid=(groups,),
        out_shape=jax.ShapeDtypeStruct((bands, rows, groups * 128), jnp.bfloat16),
        in_specs=[
            pl.BlockSpec((rows, long), lambda g: (g, 0)),
            pl.BlockSpec((side, long), lambda g: (g, 0)),
            pl.BlockSpec((side, long), lambda g: (g, 0)),
            pl.BlockSpec((1, rows, deep), lambda g: (g, 0, 0)),
            pl.BlockSpec((1, rows, 128), lambda g: (g, 0, 0)),
            pl.BlockSpec((1, 4, SUB, 128), lambda g: (g, 0, 0, 0)),
            pl.BlockSpec((1, SUB, 128), lambda g: (g, 0, 0)),
            pl.BlockSpec((2, SUB, 128), lambda g: (0, 0, 0)),
        ],
        out_specs=pl.BlockSpec((bands, rows, 128), lambda g: (0, 0, g)),
        scratch_shapes=[pltpu.VMEM((rows, long), jnp.float32)],
        name="front",
    )(own, low, high, weights, bias, taps, dil, flags)


def build_kron(mix_ref, kron_ref):
    size = kron_ref.shape[0]
    bins = size // SUB
    one = (
        lax.broadcasted_iota(jnp.int32, (size, bins), 0) // SUB
        == lax.broadcasted_iota(jnp.int32, (size, bins), 1)
    ).astype(jnp.bfloat16)
    tall = jnp.dot(one, mix_ref[...], preferred_element_type=jnp.float32).astype(jnp.bfloat16)
    wide = (
        lax.broadcasted_iota(jnp.int32, (bins, size), 1) // SUB
        == lax.broadcasted_iota(jnp.int32, (bins, size), 0)
    ).astype(jnp.bfloat16)
    kron_ref[...] = jnp.zeros_like(kron_ref)
    step = 256
    rows = lax.broadcasted_iota(jnp.int32, (step, step), 0)
    cols = lax.broadcasted_iota(jnp.int32, (step, step), 1)
    same = (rows % SUB) == (cols % SUB)
    for i in range(size // step):
        for j in range(size // step):
            part = jnp.dot(
                tall[i * step : (i + 1) * step],
                wide[:, j * step : (j + 1) * step],
                preferred_element_type=jnp.float32,
            )
            kron_ref[i * step : (i + 1) * step, j * step : (j + 1) * step] = jnp.where(
                same, part, 0.0
            ).astype(jnp.bfloat16)


def stacked(tile, groups, row):
    return jnp.concatenate(
        [tile[row * SUB : (row + 1) * SUB, g * 128 : (g + 1) * 128] for g in range(groups)], axis=0
    )


def back_chunk(chunk, some, groups, data_ref, mixed_ref, up_ref, bup_ref, down_ref, bdown_ref, gain_ref, member_ref, out_ref):
    channels = groups * SUB
    rows = some * SUB
    base = pl.multiple_of(chunk * rows, rows)
    mixed = mixed_ref[pl.ds(base, rows), :]
    normed = []
    for r in range(some):
        m = stacked(mixed, groups, r)
        dev = m - jnp.sum(m, axis=0, keepdims=True) * (1.0 / channels)
        var = jnp.sum(dev * dev, axis=0, keepdims=True) * (1.0 / channels)
        normed.append((dev * lax.rsqrt(var + 1e-05) * gain_ref[...]).astype(jnp.bfloat16))
    flat = jnp.concatenate(normed, axis=1)
    hidden = jnp.dot(up_ref[...], flat, preferred_element_type=jnp.float32)
    act = jnp.concatenate(
        [
            gelu(hidden[:, r * 128 : (r + 1) * 128] + bup_ref[...]).astype(jnp.bfloat16)
            for r in range(some)
        ],
        axis=1,
    )
    proj = jnp.dot(down_ref[...], act, preferred_element_type=jnp.float32)
    data = data_ref[pl.ds(base, rows), :].astype(jnp.float32)
    plain, square = [], []
    for r in range(some):
        block = proj[:, r * 128 : (r + 1) * 128] + bdown_ref[...] + stacked(data, groups, r)
        for value, store in ((block, plain), (block * block, square)):
            head = value.astype(jnp.bfloat16)
            tail = (value - head.astype(jnp.float32)).astype(jnp.bfloat16)
            store.append(jnp.concatenate([head, tail], axis=1))
    for k, store in enumerate((plain, square)):
        total = lax.dot_general(
            member_ref[...],
            jnp.concatenate(store, axis=0),
            (((1,), (1,)), ((), ())),
            preferred_element_type=jnp.float32,
        )
        out_ref[chunk, k] = total


def back_kernel(groups, some, data_ref, mix_ref, up_ref, bup_ref, down_ref, bdown_ref, gain_ref, member_ref, out_ref, kron_ref, mixed_ref):
    build_kron(mix_ref, kron_ref)
    size = kron_ref.shape[0]
    step = 128

    @pl.loop(0, size // step)
    def _(i):
        at = pl.multiple_of(i * step, step)
        mixed_ref[pl.ds(at, step), :] = jnp.dot(
            kron_ref[pl.ds(at, step), :], data_ref[...], preferred_element_type=jnp.float32
        )

    @pl.loop(0, size // (SUB * some))
    def _(chunk):
        back_chunk(chunk, some, groups, data_ref, mixed_ref, up_ref, bup_ref, down_ref, bdown_ref, gain_ref, member_ref, out_ref)


def back(data, w_mix, up, bup, down, bdown, gain, member, groups, some):
    size = data.shape[0]
    epochs = member.shape[0]
    bins = size // SUB
    channels = groups * SUB
    return pl.pallas_call(
        functools.partial(back_kernel, groups, some),
        out_shape=jax.ShapeDtypeStruct((bins // some, 2, epochs, some * channels), jnp.float32),
        in_specs=[pl.BlockSpec(memory_space=pltpu.VMEM)] * 8,
        out_specs=pl.BlockSpec(memory_space=pltpu.VMEM),
        scratch_shapes=[
            pltpu.VMEM((size, size), jnp.bfloat16),
            pltpu.VMEM((size, data.shape[1]), jnp.float32),
        ],
        name="back",
    )(data, w_mix, up, bup, down, bdown, gain, member)


def on_device(
    spectrum,
    w_freq,
    b_freq,
    dilation,
    w_time,
    b_time,
    w_mix,
    ln_gain,
    w_up,
    b_up,
    w_down,
    b_down,
    epoch_lengths,
):
    channels, bins, frames = spectrum.shape
    size = w_freq.shape[2]
    groups = channels // size
    bands = lax.axis_size("band")
    blocks = lax.axis_size("tm")
    tm = lax.axis_index("tm")
    long = frames + 2 * REACH
    some = bins // 2

    before = shifted(spectrum[:, :, frames - REACH :], "tm", 1)
    after = shifted(spectrum[:, :, :REACH], "tm", -1)
    longer = jnp.concatenate([before, spectrum, after], axis=2)
    low = shifted(longer[:, bins - 2 :], "band", 1).reshape(channels * 2, long)
    high = shifted(longer[:, :2], "band", -1).reshape(channels * 2, long)
    own = longer.reshape(channels * bins, long)

    weights = banded_weights(w_freq, bins)
    bias = jnp.broadcast_to(
        b_freq.reshape(groups, 1, size, 1), (groups, bins, size, 128)
    ).reshape(groups, bins * size, 128)
    taps = jnp.concatenate([w_time, b_time[None]], axis=0).reshape(4, groups, size, 1)
    taps = jnp.broadcast_to(jnp.transpose(taps, (1, 0, 2, 3)), (groups, 4, size, 128))
    dil = jnp.broadcast_to(dilation.reshape(groups, size, 1), (groups, size, 128))
    inside = jnp.stack([tm > 0, tm < blocks - 1]).astype(jnp.float32)
    flags = jnp.broadcast_to(inside[:, None, None], (2, SUB, 128))
    parts = front(own, low, high, weights, bias, taps, dil, flags, bands)

    swapped = lax.all_to_all(parts, "band", split_axis=0, concat_axis=0, tiled=True)
    data = swapped.reshape(bands * bins * size, groups * 128)

    row = epoch_lengths[0]
    epochs = row.shape[0]
    ends = jnp.cumsum(row)
    starts = ends - row
    piece = frames // bands
    ids = lax.axis_index("band") * piece + jnp.arange(piece, dtype=jnp.int32)
    member = ((ids[None, :] >= starts[:, None]) & (ids[None, :] < ends[:, None])).astype(jnp.bfloat16)
    member = jnp.concatenate([member, member], axis=1)

    def wide(x):
        return jnp.broadcast_to(x[:, None], (x.shape[0], 128))

    sums = back(data, w_mix, w_up.T, wide(b_up), w_down.T, wide(b_down), wide(ln_gain), member, groups, some)
    split = sums.reshape(bands, 2, 2, epochs, some * channels)
    got = lax.all_to_all(split, "band", split_axis=0, concat_axis=0, tiled=True)
    total = jnp.sum(got, axis=0) / row.astype(jnp.float32)[None, None, :, None]
    total = jnp.transpose(total, (1, 2, 0, 3)).reshape(2, epochs, bins * channels)
    return total[0], total[1]


def solution(mesh):
    return jax.shard_map(
        on_device,
        mesh=mesh,
        in_specs=(
            P(None, "band", "tm"),
            P(),
            P(),
            P(),
            P(),
            P(),
            P(),
            P(),
            P(),
            P(),
            P(),
            P(),
            P("tm", None),
        ),
        out_specs=(P("tm", "band"), P("tm", "band")),
        check_vma=False,
    )
```

time: 621 us -> 156 us (0.25); the launches traced: 609 us -> 155 us
  local copies, waits for them, and re-layouts: 446 us -> 42.6 us
  matrix products: 62.2 us -> 1.27 us
  Pallas kernels: 0 us -> 36.1 us
  other arithmetic: 17.2 us -> 2.76 us
  starting transfers between devices: 38.6 us -> 31.1 us
    gather x384 -> x0, local copies, waits for them, and re-layouts: 424 us -> none
    dot_general x21 -> x1, matrix products: 62.2 us -> 1.27 us  [banded_weights(): jnp.einsum('kfp,kgco->gfocp', jnp.asarray(place, jnp.bfloat16), grouped,...]
    pallas_call x0 -> x2, Pallas kernels: none -> 36.1 us  [the longest x1 27.6 us: back(): pl.pallas_call(functools.partial(back_kernel, groups, some), out_shape=ja...]
    slice x2 -> x8, local copies, waits for them, and re-layouts: 1.07 us -> 16.2 us  [the longest x2 6.82 us: banded_weights(): low = full[..., :half].reshape(channels // size, rows, size * half)]
    reshape x0 -> x8, local copies, waits for them, and re-layouts: none -> 11 us  [the longest x2 3.3 us: banded_weights(): high = full[..., half + bins:].reshape(channels // size, rows, size * half)]
    unnamed x29 -> x27, local copies, waits for them, and re-layouts: 13.1 us -> 2.91 us
    transpose x2 -> x0, other arithmetic: 9.44 us -> none  [the longest x1 9.4 us: on_device(): jnp.transpose(filtered.reshape(channels, local_bins, bands, piece), (2, 0...]
    all_to_all x1, starting transfers between devices: 16.5 us -> 9.73 us  [on_device(): lax.all_to_all(parts, 'band', split_axis=0, concat_axis=0, tiled=True)]
  transfers between devices with their start and end apart: 6 -> 6, of which waited for: 2 -> 2; matrix products, arithmetic and copies ran while one was open for 1% -> 23% of each run, Pallas kernels for 0% -> 0%
where the time goes in v2:
time: 156 us; the launch traced here: 155 us
  local copies, waits for them, and re-layouts  42.6 us (27%)
  waiting for transfers between devices  39.9 us (26%)
  Pallas kernels  36.1 us (23%)
  starting transfers between devices  31.1 us (20%)
  other arithmetic  2.76 us (2%)
    pallas_call x1, Pallas kernels, back(): pl.pallas_call(functools.partial(back_kernel, groups, some), out_shape=ja...  27.6 us
    all_to_all x1, waiting for transfers between devices, on_device(): lax.all_to_all(parts, 'band', split_axis=0, concat_axis=0, tiled=True)  27.6 us
    ppermute x4, starting transfers between devices, shifted(): return lax.ppermute(block, axis, pairs)  16.8 us
    all_to_all x1, waiting for transfers between devices, on_device(): got = lax.all_to_all(split, 'band', split_axis=0, concat_axis=0, tiled=True)  12.3 us
    all_to_all x1, starting transfers between devices, on_device(): lax.all_to_all(parts, 'band', split_axis=0, concat_axis=0, tiled=True)  9.73 us
    pallas_call x1, Pallas kernels, front(): pl.pallas_call(functools.partial(front_kernel, bands), grid=(groups,), ou...  8.46 us
    slice x2, local copies, waits for them, and re-layouts, banded_weights(): low = full[..., :half].reshape(channels // size, rows, size * half)  6.82 us
    slice x1, local copies, waits for them, and re-layouts, banded_weights(): high = full[..., half + bins:].reshape(channels // size, rows, size * half)  5.03 us
  transfers between devices with their start and end apart: 6, of which 2 were waited for; matrix products, arithmetic and copies ran while one was open for 23% of the time, Pallas kernels for 0%

profile of v2, /device:TPU:8, one launch (start us, length us, event | category | flops | bytes accessed | tf_op | source)
XLA Modules:
  0.0 154.6 jit_solution(15898175553926216957)
XLA Ops:
  0.6 1.0 fusion.2
  1.7 3.8 %collective-permute-start = (bf16[64,8,128]{2,0,1:T(8,128)(2,1)S(1)}, bf16[64,8,128]{2,0,1:T(8,128)(2,1)}, u32[]{:S(2)}, u32[]{:S(2)}) collective-permute-start(bf16[64,8,128]{2,0,1:T(8,128)(2,1)S(1)} %copy.51), channel_id=1, source_target_pairs={{0,1},{1,2},{2,3},{3,4},{4,5},{5,6},{6,7},{7,8},{8,9},{9,10},{10,1... | collective-permute-start | bytes 393224 | tf_op jit(solution)/shard_map/ppermute | solution.py:26
  5.5 9.4 %collective-permute-start.1 = (bf16[64,8,128]{2,0,1:T(8,128)(2,1)S(1)}, bf16[64,8,128]{2,0,1:T(8,128)(2,1)}, u32[]{:S(2)}, u32[]{:S(2)}) collective-permute-start(bf16[64,8,128]{2,0,1:T(8,128)(2,1)S(1)} %copy.52), channel_id=1, source_target_pairs={{1,0},{2,1},{3,2},{4,3},{5,4},{6,5},{7,6},{8,7},{9,8},{10,9},{11,1... | collective-permute-start | bytes 393224 | tf_op jit(solution)/shard_map/ppermute | solution.py:26
  14.9 0.9 copy.48
  15.8 1.3 fusion
  17.1 0.4 slice.42
  17.5 0.9 constant_dynamic-update-slice_fusion.2
  18.4 1.2 constant_dynamic-update-slice_fusion.1
  19.6 0.9 constant_dynamic-update-slice_fusion
  20.5 1.1 fusion.1
  21.6 2.3 %collective-permute-start.2 = (bf16[64,2,2304]{2,0,1:T(8,128)(2,1)}, bf16[64,2,2304]{2,0,1:T(8,128)(2,1)}, u32[]{:S(2)}, u32[]{:S(2)}) collective-permute-start(bf16[64,2,2304]{2,0,1:T(8,128)(2,1)} %get-tuple-element.3), channel_id=1, source_target_pairs={{0,32},{32,64},{64,96},{96,128},{128,160},{160,192},{192,224},{224... | collective-permute-start | bytes 1769480 | tf_op jit(solution)/shard_map/ppermute | solution.py:26
  23.9 1.3 collective-permute-start.3
  25.2 1.8 %fusion.3 = (bf16[8,8,8,8,2]{4,2,3,0,1:T(8,128)(2,1)}, bf16[8,8,8,8,2]{4,2,3,0,1:T(8,128)(2,1)}) fusion(bf16[8,8,8,8,12]{4,2,3,0,1:T(8,128)(2,1)S(1)} %fusion), kind=kLoop, calls=%fused_computation.17 | loop fusion | bytes 65536 | tf_op jit(solution)/shard_map/slice | solution.py:45
  27.0 5.0 %copy.40 = bf16[8,8,8,8,2]{2,1,4,3,0:T(8,128)(2,1)} copy(bf16[8,8,8,8,2]{4,2,3,0,1:T(8,128)(2,1)} %get-tuple-element.6) | data formatting | bytes 32768 | tf_op jit(solution)/shard_map/slice | solution.py:45
  32.0 1.8 %reshape.107 = bf16[8,64,16]{1,2,0:T(8,128)(2,1)} reshape(bf16[8,8,8,8,2]{2,1,4,3,0:T(8,128)(2,1)} %copy.40) | data formatting | bytes 32768 | tf_op jit(solution)/shard_map/reshape | solution.py:45
  33.8 0.9 copy.42
  34.7 5.0 %copy.41 = bf16[8,8,8,8,2]{2,1,4,3,0:T(8,128)(2,1)} copy(bf16[8,8,8,8,2]{4,2,3,0,1:T(8,128)(2,1)} %get-tuple-element.7) | data formatting | bytes 32768 | tf_op jit(solution)/shard_map/slice | solution.py:46
  39.8 1.8 %reshape.108 = bf16[8,64,16]{1,2,0:T(8,128)(2,1)} reshape(bf16[8,8,8,8,2]{2,1,4,3,0:T(8,128)(2,1)} %copy.41) | data formatting | bytes 32768 | tf_op jit(solution)/shard_map/reshape | solution.py:46
  41.5 1.5 copy.43
  43.1 1.3 copy.39
  44.3 2.0 %reshape.106 = bf16[8,64,64]{2,1,0:T(8,128)(2,1)S(1)} reshape(bf16[8,8,8,8,8]{4,3,2,1,0:T(8,128)(2,1)} %copy.39) | data formatting | bytes 131072 | tf_op jit(solution)/shard_map/reshape | solution.py:44
  46.4 0.1 broadcast_in_dim.24
  46.5 0.1 broadcast_in_dim.26
  46.5 0.1 concatenate.25
  46.8 0.1 add_convert_fusion.1
  46.9 1.7 %pad_maximum_fusion.w_ref = bf16[8,64,96]{2,1,0:T(8,128)(2,1)} fusion(bf16[8,64,16]{2,1,0:T(8,128)(2,1)} %copy.43, bf16[8,64,16]{2,1,0:T(8,128)(2,1)S(1)} %copy.42, bf16[8,64,64]{2,1,0:T(8,128)(2,1)S(1)} %reshape.106), kind=kLoop, calls=%fused_computation.3 | loop fusion | flops 294912 | bytes 196608 | tf_op jit(solution)/shard_map/concatenate | solution.py:47
  48.6 2.7 %copy.53 = bf16[64,8,2304]{2,1,0:T(8,128)(2,1)} copy(bf16[64,8,2304]{2,0,1:T(8,128)(2,1)S(1)} %constant_dynamic-update-slice_fusion) | data formatting | bytes 4718592 | tf_op jit(solution)/shard_map/concatenate | solution.py:252
  51.3 1.7 %copy.36 = bf16[64,2,2304]{2,1,0:T(2,128)(2,1)S(1)} copy(bf16[64,2,2304]{2,0,1:T(8,128)(2,1)} %collective-permute-done.2) | data formatting | bytes 1179648 | tf_op jit(solution)/shard_map/ppermute | solution.py:26
  53.0 1.0 reshape.103.low_ref
  54.0 1.7 %copy.37 = bf16[64,2,2304]{2,1,0:T(2,128)(2,1)S(1)} copy(bf16[64,2,2304]{2,0,1:T(8,128)(2,1)} %collective-permute-done.3) | data formatting | bytes 1179648 | tf_op jit(solution)/shard_map/ppermute | solution.py:26
  55.7 1.1 reshape.104.high_ref
  56.8 0.7 broadcast_in_dim.63.flag_ref
  57.4 0.8 broadcast_in_dim.27.b_ref
  58.3 0.8 broadcast_in_dim.29.taps_ref
  59.0 0.7 broadcast_in_dim.62.dil_ref
  59.7 8.5 %front.1 = bf16[16,64,1024]{2,1,0:T(8,128)(2,1)} custom-call(bf16[512,2304]{1,0:T(8,128)(2,1)} %bitcast.44, bf16[128,2304]{1,0:T(8,128)(2,1)} %reshape.103.low_ref, bf16[128,2304]{1,0:T(8,128)(2,1)} %reshape.104.high_ref, bf16[8,64,96]{2,1,0:T(8,128)(2,1)} %pad_maximum_fusion.w_ref, f32[8,64,128]{2,1,0:T(8,128)} %broadcast_in_dim.27.b_ref, ...), custom_call_target="tpu_custom_call" | custom-call | tf_op jit(solution)/shard_map/front/pallas_call | solution.py:97
  68.2 9.7 %all-to-all-start = ((bf16[16,64,1024]{2,1,0:T(8,128)(2,1)}), bf16[16,64,1024]{2,1,0:T(8,128)(2,1)S(1)}, u32[]{:S(2)}, u32[]{:S(2)}) async-start(bf16[16,64,1024]{2,1,0:T(8,128)(2,1)} %front.1), calls=%async_computation | async-start | bytes 4194304 | tf_op jit(solution)/shard_map/all_to_all | solution.py:268
  78.0 0.2 reduce-window.7
  78.2 0.7 copy.46
  79.0 0.6 add_convert_fusion.member_ref
  79.6 27.6 %all-to-all-done = bf16[16,64,1024]{2,1,0:T(8,128)(2,1)S(1)} async-done(((bf16[16,64,1024]{2,1,0:T(8,128)(2,1)}), bf16[16,64,1024]{2,1,0:T(8,128)(2,1)S(1)}, u32[]{:S(2)}, u32[]{:S(2)}) %all-to-all-start) | async-done | bytes 2097184 | tf_op jit(solution)/shard_map/all_to_all | solution.py:268
  107.1 0.8 broadcast_in_dim.64.bup_ref
  108.0 0.7 broadcast_in_dim.65.bdown_ref
  108.7 0.7 broadcast_in_dim.66.gain_ref
  109.4 27.6 %back.1 = f32[32,2,8,256]{3,2,1,0:T(8,128)} custom-call(bf16[1024,1024]{1,0:T(8,128)(2,1)} %bitcast.45, bf16[128,128]{1,0:T(8,128)(2,1)} %mix_ref.1, bf16[256,64]{1,0:T(8,128)(2,1)} %bitcast.48, f32[256,128]{1,0:T(8,128)} %broadcast_in_dim.64.bup_ref, bf16[64,256]{1,0:T(8,128)(2,1)} %bitcast.49, f32[64,128]{1,0:T(8,128)} %broadcast_in_dim.65.bdown_ref, ...), custom_call_target="tpu_custom_call" | custom-call | tf_op jit(solution)/shard_map/back/pallas_call | solution.py:213
  137.0 4.6 %all-to-all-start.1 = ((f32[16,2,2,8,256]{4,3,2,1,0:T(8,128)}), f32[16,2,2,8,256]{4,3,2,1,0:T(8,128)S(1)}, u32[]{:S(2)}, u32[]{:S(2)}) async-start(f32[16,2,2,8,256]{4,3,2,1,0:T(8,128)} %bitcast.46), calls=%async_computation.1 | async-start | bytes 1048576 | tf_op jit(solution)/shard_map/all_to_all | solution.py:285
  141.6 12.3 %all-to-all-done.1 = f32[16,2,2,8,256]{4,3,2,1,0:T(8,128)S(1)} async-done(((f32[16,2,2,8,256]{4,3,2,1,0:T(8,128)}), f32[16,2,2,8,256]{4,3,2,1,0:T(8,128)S(1)}, u32[]{:S(2)}, u32[]{:S(2)}) %all-to-all-start.1) | async-done | bytes 524320 | tf_op jit(solution)/shard_map/all_to_all | solution.py:285
  154.0 0.6 fusion.4
  (39 shorter events, 0.5 us)
Async XLA Ops:
  1.7 15.8 %collective-permute-start = (bf16[64,8,128]{2,0,1:T(8,128)(2,1)S(1)}, bf16[64,8,128]{2,0,1:T(8,128)(2,1)}, u32[]{:S(2)}, u32[]{:S(2)}) collective-permute-start(bf16[64,8,128]{2,0,1:T(8,128)(2,1)S(1)} %copy.51), channel_id=1, source_target_pairs={{0,1},{1,2},{2,3},{3,4},{4,5},{5,6},{6,7},{7,8},{8,9},{9,10},{10,1... | collective-permute-start | bytes 393224 | tf_op jit(solution)/shard_map/ppermute | solution.py:26
  5.5 14.1 %collective-permute-start.1 = (bf16[64,8,128]{2,0,1:T(8,128)(2,1)S(1)}, bf16[64,8,128]{2,0,1:T(8,128)(2,1)}, u32[]{:S(2)}, u32[]{:S(2)}) collective-permute-start(bf16[64,8,128]{2,0,1:T(8,128)(2,1)S(1)} %copy.52), channel_id=1, source_target_pairs={{1,0},{2,1},{3,2},{4,3},{5,4},{6,5},{7,6},{8,7},{9,8},{10,9},{11,1... | collective-permute-start | bytes 393224 | tf_op jit(solution)/shard_map/ppermute | solution.py:26
  15.8 2.6 %copy-start.1 = (bf16[64,8,2048]{2,1,0:T(8,128)(2,1)S(1)}, bf16[64,8,2048]{2,1,0:T(8,128)(2,1)}, u32[]{:S(2)}) copy-start(bf16[64,8,2048]{2,1,0:T(8,128)(2,1)} %param.14) | copy-start | bytes 6291460
  21.6 29.7 %collective-permute-start.2 = (bf16[64,2,2304]{2,0,1:T(8,128)(2,1)}, bf16[64,2,2304]{2,0,1:T(8,128)(2,1)}, u32[]{:S(2)}, u32[]{:S(2)}) collective-permute-start(bf16[64,2,2304]{2,0,1:T(8,128)(2,1)} %get-tuple-element.3), channel_id=1, source_target_pairs={{0,32},{32,64},{64,96},{96,128},{128,160},{160,192},{192,224},{224... | collective-permute-start | bytes 1769480 | tf_op jit(solution)/shard_map/ppermute | solution.py:26
  23.9 30.1 %collective-permute-start.3 = (bf16[64,2,2304]{2,0,1:T(8,128)(2,1)}, bf16[64,2,2304]{2,0,1:T(8,128)(2,1)}, u32[]{:S(2)}, u32[]{:S(2)}) collective-permute-start(bf16[64,2,2304]{2,0,1:T(8,128)(2,1)} %get-tuple-element.2), channel_id=1, source_target_pairs={{32,0},{64,32},{96,64},{128,96},{160,128},{192,160},{224,192},{256... | collective-permute-start | bytes 1769480 | tf_op jit(solution)/shard_map/ppermute | solution.py:26
  34.7 11.7 %copy-start.7 = (f32[64]{0:T(128)S(1)}, f32[64]{0:T(128)}, u32[]{:S(2)}) copy-start(f32[64]{0:T(128)} %param.16) | copy-start | bytes 772
  34.7 11.8 %copy-start.3 = (f32[3,64]{1,0:T(4,128)S(1)}, f32[3,64]{1,0:T(4,128)}, u32[]{:S(2)}) copy-start(f32[3,64]{1,0:T(4,128)} %param.18) | copy-start | bytes 2308
  34.7 11.9 %copy-start.8 = (f32[64]{0:T(128)S(1)}, f32[64]{0:T(128)}, u32[]{:S(2)}) copy-start(f32[64]{0:T(128)} %param.19) | copy-start | bytes 772
  34.7 12.0 %copy-start.9 = (s32[64]{0:T(128)S(1)}, s32[64]{0:T(128)}, u32[]{:S(2)}) copy-start(s32[64]{0:T(128)} %param.17) | copy-start | bytes 772
  68.2 9.8 %copy-start.10 = (s32[1,8]{1,0:T(1,128)S(1)}, s32[1,8]{1,0:T(1,128)}, u32[]{:S(2)}) copy-start(s32[1,8]{1,0:T(1,128)} %param.26) | copy-start | bytes 100
  68.2 10.0 %copy-start.2 = (bf16[64,256]{1,0:T(8,128)(2,1)S(1)}, bf16[64,256]{1,0:T(8,128)(2,1)}, u32[]{:S(2)}) copy-start(bf16[64,256]{1,0:T(8,128)(2,1)} %param.22) | copy-start | bytes 98308
  68.2 39.0 %copy-start.4 = (f32[256]{0:T(256)S(1)}, f32[256]{0:T(256)}, u32[]{:S(2)}) copy-start(f32[256]{0:T(256)} %param.23) | copy-start | bytes 3076
  68.2 39.8 %copy-start.5 = (f32[64]{0:T(128)S(1)}, f32[64]{0:T(128)}, u32[]{:S(2)}) copy-start(f32[64]{0:T(128)} %param.25) | copy-start | bytes 772
  68.2 40.5 %copy-start.6 = (f32[64]{0:T(128)S(1)}, f32[64]{0:T(128)}, u32[]{:S(2)}) copy-start(f32[64]{0:T(128)} %param.21) | copy-start | bytes 772
  68.2 38.9 %all-to-all-start = ((bf16[16,64,1024]{2,1,0:T(8,128)(2,1)}), bf16[16,64,1024]{2,1,0:T(8,128)(2,1)S(1)}, u32[]{:S(2)}, u32[]{:S(2)}) async-start(bf16[16,64,1024]{2,1,0:T(8,128)(2,1)} %front.1), calls=%async_computation | async-start | bytes 4194304 | tf_op jit(solution)/shard_map/all_to_all | solution.py:268
  107.1 2.2 %copy-start = (bf16[16,64,1024]{2,1,0:T(8,128)(2,1)}, bf16[16,64,1024]{2,1,0:T(8,128)(2,1)S(1)}, u32[]{:S(2)}) copy-start(bf16[16,64,1024]{2,1,0:T(8,128)(2,1)S(1)} %all-to-all-done) | copy-start | bytes 6291460
  137.0 16.9 %all-to-all-start.1 = ((f32[16,2,2,8,256]{4,3,2,1,0:T(8,128)}), f32[16,2,2,8,256]{4,3,2,1,0:T(8,128)S(1)}, u32[]{:S(2)}, u32[]{:S(2)}) async-start(f32[16,2,2,8,256]{4,3,2,1,0:T(8,128)} %bitcast.46), calls=%async_computation.1 | async-start | bytes 1048576 | tf_op jit(solution)/shard_map/all_to_all | solution.py:285

commit v3 on v2

v3 whole, which is shorter than its diff:
```python
import functools

import jax
import jax.numpy as jnp
from jax import lax
from jax.experimental import pallas as pl
from jax.experimental.pallas import tpu as pltpu
from jax.sharding import PartitionSpec as P

MESH = pl.DeviceIdType.MESH
REACH = 128
SUB = 8
GELU_C = 0.7978845608028654
GELU_A = 0.044715


def gelu(x):
    inner = x * (GELU_C + (GELU_C * GELU_A) * (x * x))
    half = 0.5 * x
    return half + half * jnp.tanh(inner)


def build_kron(mix_ref, kron_ref):
    size = kron_ref.shape[0]
    bins = size // SUB
    one = (
        lax.broadcasted_iota(jnp.int32, (size, bins), 0) // SUB
        == lax.broadcasted_iota(jnp.int32, (size, bins), 1)
    ).astype(jnp.bfloat16)
    tall = jnp.dot(one, mix_ref[...], preferred_element_type=jnp.float32).astype(jnp.bfloat16)
    wide = (
        lax.broadcasted_iota(jnp.int32, (bins, size), 1) // SUB
        == lax.broadcasted_iota(jnp.int32, (bins, size), 0)
    ).astype(jnp.bfloat16)
    kron_ref[...] = jnp.zeros_like(kron_ref)
    step = 256
    rows = lax.broadcasted_iota(jnp.int32, (step, step), 0)
    cols = lax.broadcasted_iota(jnp.int32, (step, step), 1)
    same = (rows % SUB) == (cols % SUB)
    for i in range(size // step):
        for j in range(size // step):
            part = jnp.dot(
                tall[i * step : (i + 1) * step],
                wide[:, j * step : (j + 1) * step],
                preferred_element_type=jnp.float32,
            )
            kron_ref[i * step : (i + 1) * step, j * step : (j + 1) * step] = jnp.where(
                same, part, 0.0
            ).astype(jnp.bfloat16)


def stacked3(tile, groups, row):
    return jnp.concatenate([tile[g, row * SUB : (row + 1) * SUB, :] for g in range(groups)], axis=0)


def stacked(tile, groups, row):
    return jnp.concatenate(
        [tile[row * SUB : (row + 1) * SUB, g * 128 : (g + 1) * 128] for g in range(groups)], axis=0
    )


def back_chunk(chunk, some, groups, data_ref, mixed_ref, up_ref, bup_ref, down_ref, bdown_ref, gain_ref, member_ref):
    channels = groups * SUB
    rows = some * SUB
    base = pl.multiple_of(chunk * rows, rows)
    mixed = mixed_ref[pl.ds(base, rows), :]
    normed = []
    for r in range(some):
        m = stacked(mixed, groups, r)
        dev = m - jnp.sum(m, axis=0, keepdims=True) * (1.0 / channels)
        var = jnp.sum(dev * dev, axis=0, keepdims=True) * (1.0 / channels)
        normed.append((dev * lax.rsqrt(var + 1e-05) * gain_ref[...]).astype(jnp.bfloat16))
    flat = jnp.concatenate(normed, axis=1)
    hidden = jnp.dot(up_ref[...], flat, preferred_element_type=jnp.float32)
    act = jnp.concatenate(
        [
            gelu(hidden[:, r * 128 : (r + 1) * 128] + bup_ref[...]).astype(jnp.bfloat16)
            for r in range(some)
        ],
        axis=1,
    )
    proj = jnp.dot(down_ref[...], act, preferred_element_type=jnp.float32)
    data = data_ref[:, pl.ds(base, rows), :].astype(jnp.float32)
    plain, square = [], []
    for r in range(some):
        block = proj[:, r * 128 : (r + 1) * 128] + bdown_ref[...] + stacked3(data, groups, r)
        for value, store in ((block, plain), (block * block, square)):
            head = value.astype(jnp.bfloat16)
            tail = (value - head.astype(jnp.float32)).astype(jnp.bfloat16)
            store.append(jnp.concatenate([head, tail], axis=1))
    return [
        lax.dot_general(
            member_ref[...],
            jnp.concatenate(store, axis=0),
            (((1,), (1,)), ((), ())),
            preferred_element_type=jnp.float32,
        )
        for store in (plain, square)
    ]


def column(row, first, count):
    lane = lax.broadcasted_iota(jnp.int32, (count, row.shape[1]), 1)
    sub = lax.broadcasted_iota(jnp.int32, (count, row.shape[1]), 0)
    picked = jnp.where(lane == sub + first, jnp.broadcast_to(row, lane.shape), 0.0)
    return jnp.sum(picked, axis=1, keepdims=True)


def wide(col):
    return jnp.broadcast_to(col, (col.shape[0], 128))


def edge_picker(bins):
    shape = (4 * SUB, SUB * bins)
    row = lax.broadcasted_iota(jnp.int32, shape, 0)
    col = lax.broadcasted_iota(jnp.int32, shape, 1)
    edge = row % 2 + jnp.where(row >= 2 * SUB, bins - 2, 0)
    channel = (row % (2 * SUB)) // 2
    return (col == channel * bins + edge).astype(jnp.bfloat16)


def group_weights(wt_ref, g, bins, low_on, high_on):
    taps, size, channels = wt_ref.shape
    long = bins + taps - 1
    row = lax.broadcasted_iota(jnp.int32, (channels, 128), 0)
    q = lax.broadcasted_iota(jnp.int32, (channels, 128), 1)
    pick = ((row == g * size + q // long) & (q < size * long)).astype(jnp.bfloat16)
    spread = [
        jnp.dot(wt_ref[k], pick, preferred_element_type=jnp.float32) for k in range(taps)
    ]
    place = lax.broadcasted_iota(jnp.int32, (size, 128), 1) % long
    base = jnp.zeros((size, 128), jnp.float32)
    for k in range(taps):
        base = jnp.where(place == k, spread[k], base)
    turned = [base] + [pltpu.roll(base, f, 1) for f in range(1, bins)]
    big = jnp.concatenate(turned, axis=0).astype(jnp.bfloat16)
    wid = size * long
    p = lax.broadcasted_iota(jnp.int32, (128, wid), 1)
    src = lax.broadcasted_iota(jnp.int32, (128, wid), 0)
    inner = size * bins
    lo = p - inner
    hi = lo - 2 * size
    wanted = jnp.where(
        p < inner,
        (p // bins) * long + p % bins + 2,
        jnp.where(
            lo < 2 * size,
            (lo // 2) * long + lo % 2 + jnp.where(low_on, 0, 4096),
            (hi // 2) * long + bins + 2 + hi % 2 + jnp.where(high_on, 0, 4096),
        ),
    )
    order = (src == wanted).astype(jnp.bfloat16)
    return jnp.dot(big, order, preferred_element_type=jnp.float32).astype(jnp.bfloat16)


def front_group(g, bands, weights, own_ref, ends_ref, low_ref, high_ref, cor_ref, rows_of, before_on, after_on, spec_ref, send_ref):
    rows = weights.shape[0]
    long = own_ref.shape[1]
    tiles = long // 128 + 2
    at = pl.multiple_of(g * rows, rows)
    small = pl.multiple_of(g * 16, 16)
    body = jnp.concatenate(
        [own_ref[pl.ds(at, rows), :], low_ref[pl.ds(small, 16), :], high_ref[pl.ds(small, 16), :]],
        axis=0,
    )
    first, last = (
        jnp.concatenate(
            [
                ends_ref[i, pl.ds(at, rows), :],
                cor_ref[i, 0, pl.ds(small, 16), :],
                cor_ref[i, 1, pl.ds(small, 16), :],
            ],
            axis=0,
        )
        for i in range(2)
    )
    data = jnp.concatenate([first, body, last], axis=1)
    pre = jnp.dot(weights, data, preferred_element_type=jnp.float32)
    t0, t1, t2, shift, bias8, step = (wide(column(r, g * SUB, SUB)) for r in rows_of)
    bias = jnp.concatenate([bias8] * (rows // SUB), axis=0)
    step = step.astype(jnp.int32)
    for j in range(tiles):
        cols = slice(j * 128, (j + 1) * 128)
        act = gelu(pre[:, cols] + bias)
        if j == 0:
            act = act * before_on
        if j == tiles - 1:
            act = act * after_on
        spec_ref[:, cols] = act.astype(jnp.bfloat16).astype(jnp.float32)
    lane = lax.broadcasted_iota(jnp.int32, (SUB, 128), 1)
    from_left = (lane - step) & 127
    from_right = (lane + step) & 127
    keep_left = lane >= step
    keep_right = lane + step < 128

    def take(value, index):
        return jnp.take_along_axis(value, index, axis=1, mode="promise_in_bounds")

    def half(start):
        v = [spec_ref[start : start + SUB, j * 128 : (j + 1) * 128] for j in range(tiles)]
        left = [take(v[j], from_left) for j in range(tiles - 1)]
        right = [take(v[j], from_right) for j in range(1, tiles)]
        outs = []
        for j in range(1, tiles - 1):
            a = jnp.where(keep_left, left[j], left[j - 1])
            c = jnp.where(keep_right, right[j - 1], right[j])
            outs.append(t0 * a + t1 * v[j] + t2 * c + shift)
        return outs

    for pair in range(rows // 16):
        top = half(pair * 16)
        bottom = half(pair * 16 + SUB)
        for j in range(bands):
            both = jnp.concatenate([top[j], bottom[j]], axis=0)
            send_ref[g, j, pair * 16 : (pair + 1) * 16, :] = both.astype(jnp.bfloat16)


def kernel(
    bands,
    blocks,
    bins,
    some,
    own_ref,
    wt_ref,
    bfreq_ref,
    dil_ref,
    wtime_ref,
    btime_ref,
    mix_ref,
    gain_in,
    up_in,
    bup_in,
    down_ref,
    bdown_in,
    lens_ref,
    mean_ref,
    power_ref,
    ends_ref,
    plow_ref,
    phigh_ref,
    low_ref,
    high_ref,
    cor_ref,
    spec_ref,
    send_ref,
    data_ref,
    kron_ref,
    mixed_ref,
    part_ref,
    got_ref,
    up_ref,
    bup_ref,
    bdown_ref,
    gain_ref,
    member_ref,
    frame_sem,
    bin_sem,
    corner_sem,
    chunk_send,
    chunk_recv,
    local_sem,
    sum_send,
    sum_recv,
):
    me = lax.axis_index("band")
    tm = lax.axis_index("tm")
    channels = wt_ref.shape[2]
    groups = channels // SUB
    frames = own_ref.shape[1]
    rows = bins * SUB
    size = kron_ref.shape[0]

    def around(value, count):
        return lax.rem(value + count, count)

    up_tm, down_tm = around(tm + 1, blocks), around(tm - 1, blocks)
    up_band, down_band = around(me + 1, bands), around(me - 1, bands)

    barrier = pltpu.get_barrier_semaphore()

    @pl.loop(1, bands)
    def _(s):
        pl.semaphore_signal(barrier, inc=1, device_id={"band": lax.rem(me + s, bands), "tm": tm}, device_id_type=MESH)

    for t in (up_tm, down_tm):
        for b in (me, up_band, down_band):
            pl.semaphore_signal(barrier, inc=1, device_id={"band": b, "tm": t}, device_id_type=MESH)
    picker = edge_picker(bins)

    @pl.loop(0, groups)
    def _(g):
        at = pl.multiple_of(g * rows, rows)
        small = pl.multiple_of(g * 16, 16)
        edges = jnp.dot(picker, own_ref[pl.ds(at, rows), :], preferred_element_type=jnp.float32)
        plow_ref[pl.ds(small, 16), :] = edges[:16].astype(jnp.bfloat16)
        phigh_ref[pl.ds(small, 16), :] = edges[16:].astype(jnp.bfloat16)

    pl.semaphore_wait(barrier, bands - 1 + 6)

    def remote(src, dst, send, recv, band, block):
        return pltpu.make_async_remote_copy(
            src_ref=src,
            dst_ref=dst,
            send_sem=send,
            recv_sem=recv,
            device_id={"band": band, "tm": block},
            device_id_type=MESH,
        )

    begin, finish = pl.ds(0, 128), pl.ds(frames - 128, 128)
    small_copies = [
        remote(own_ref.at[:, finish], ends_ref.at[0], frame_sem.at[0, 0], frame_sem.at[0, 1], me, up_tm),
        remote(own_ref.at[:, begin], ends_ref.at[1], frame_sem.at[1, 0], frame_sem.at[1, 1], me, down_tm),
    ]
    k = 0
    for i, (lanes, block) in enumerate(((finish, up_tm), (begin, down_tm))):
        for h, (pack, band) in enumerate(((phigh_ref, up_band), (plow_ref, down_band))):
            small_copies.append(
                remote(pack.at[:, lanes], cor_ref.at[i, h], corner_sem.at[k, 0], corner_sem.at[k, 1], band, block)
            )
            k += 1

    def bin_copies(g):
        span = pl.ds(pl.multiple_of(g * 16, 16), 16)
        return (
            remote(phigh_ref.at[span, :], low_ref.at[span, :], bin_sem.at[g, 0, 0], bin_sem.at[g, 0, 1], up_band, tm),
            remote(plow_ref.at[span, :], high_ref.at[span, :], bin_sem.at[g, 1, 0], bin_sem.at[g, 1, 1], down_band, tm),
        )

    for copy in small_copies:
        copy.start()

    @pl.loop(0, groups)
    def _(g):
        for copy in bin_copies(g):
            copy.start()

    def chunk_out(g, s):
        there = lax.rem(me + s, bands)
        place = pl.ds(pl.multiple_of(me * rows, rows), rows)
        return remote(send_ref.at[g, there], data_ref.at[g, place, :], chunk_send.at[g, s], chunk_recv.at[g, s], there, tm)

    def chunk_in(g, s):
        there = lax.rem(me + bands - s, bands)
        place = pl.ds(pl.multiple_of(there * rows, rows), rows)
        return remote(send_ref.at[g, there], data_ref.at[g, place, :], chunk_send.at[g, s], chunk_recv.at[g, s], there, tm)

    def chunk_here(g):
        place = pl.ds(pl.multiple_of(me * rows, rows), rows)
        return pltpu.make_async_copy(send_ref.at[g, me], data_ref.at[g, place, :], local_sem.at[g])

    before_on = jnp.where(tm > 0, 1.0, 0.0).astype(jnp.float32)
    after_on = jnp.where(tm < blocks - 1, 1.0, 0.0).astype(jnp.float32)
    rows_of = (
        wtime_ref[0:1],
        wtime_ref[1:2],
        wtime_ref[2:3],
        btime_ref[...],
        bfreq_ref[...],
        dil_ref[...].astype(jnp.float32),
    )
    for copy in small_copies:
        copy.wait_recv()

    @pl.loop(0, groups)
    def _(g):
        weights = group_weights(wt_ref, g, bins, me > 0, me < bands - 1)
        for copy in bin_copies(g):
            copy.wait_recv()
        front_group(g, bands, weights, own_ref, ends_ref, low_ref, high_ref, cor_ref, rows_of, before_on, after_on, spec_ref, send_ref)

        @pl.loop(1, bands)
        def _(s):
            chunk_out(g, s).start()

        chunk_here(g).start()

    build_kron(mix_ref, kron_ref)
    up_ref[...] = up_in[...].astype(jnp.float32).T.astype(jnp.bfloat16)
    bup_ref[...] = wide(column(bup_in[...], 0, bup_ref.shape[0]))
    bdown_ref[...] = wide(column(bdown_in[...], 0, channels))
    gain_ref[...] = wide(column(gain_in[...], 0, channels))
    lens = lens_ref[...].astype(jnp.float32)
    epochs = lens.shape[1]
    eye_r = lax.broadcasted_iota(jnp.int32, (epochs, epochs), 0)
    eye_c = lax.broadcasted_iota(jnp.int32, (epochs, epochs), 1)
    all_lens = jnp.broadcast_to(lens, (epochs, epochs))
    own_len = jnp.sum(jnp.where(eye_r == eye_c, all_lens, 0.0), axis=1, keepdims=True)
    starts = jnp.sum(jnp.where(eye_c < eye_r, all_lens, 0.0), axis=1, keepdims=True)
    ids = (me * 128 + lax.broadcasted_iota(jnp.int32, (epochs, 128), 1)).astype(jnp.float32)
    member = jnp.where((ids >= starts) & (ids < starts + own_len), 1.0, 0.0)
    member_ref[...] = jnp.concatenate([member, member], axis=1).astype(jnp.bfloat16)

    @pl.loop(0, groups // 2)
    def _(p):
        for g in (2 * p, 2 * p + 1):
            chunk_here(g).wait()

            @pl.loop(1, bands)
            def _(s):
                chunk_in(g, s).wait_recv()

        cols = pl.ds(pl.multiple_of(p * 256, 256), 256)
        both = jnp.concatenate([data_ref[2 * p], data_ref[2 * p + 1]], axis=1)
        step = 256
        for i in range(size // step):
            mixed_ref[i * step : (i + 1) * step, cols] = jnp.dot(
                kron_ref[i * step : (i + 1) * step, :], both, preferred_element_type=jnp.float32
            )

    def sum_out(s):
        there = lax.rem(me + s, bands)
        return remote(part_ref.at[there], got_ref.at[me], sum_send.at[s], sum_recv.at[s], there, tm)

    def sum_in(s):
        there = lax.rem(me + bands - s, bands)
        return remote(part_ref.at[there], got_ref.at[there], sum_send.at[s], sum_recv.at[s], there, tm)

    @pl.loop(1, bands + 1)
    def _(s):
        there = lax.rem(me + s, bands)
        for half in range(bins // some):
            results = back_chunk(
                there * (bins // some) + half, some, groups, data_ref, mixed_ref, up_ref, bup_ref, down_ref, bdown_ref, gain_ref, member_ref
            )
            for k in range(2):
                part_ref[there, k, :, half * some * channels : (half + 1) * some * channels] = results[k]

        @pl.when(s < bands)
        def _():
            sum_out(s).start()

    mean_ref[...] = part_ref[me, 0]
    power_ref[...] = part_ref[me, 1]

    @pl.loop(1, bands)
    def _(s):
        sum_in(s).wait_recv()
        there = lax.rem(me + bands - s, bands)
        mean_ref[...] += got_ref[there, 0]
        power_ref[...] += got_ref[there, 1]

    mean_ref[...] = mean_ref[...] / own_len
    power_ref[...] = power_ref[...] / own_len

    for copy in small_copies:
        copy.wait_send()

    @pl.loop(0, groups)
    def _(g):
        for copy in bin_copies(g):
            copy.wait_send()

        @pl.loop(1, bands)
        def _(s):
            chunk_out(g, s).wait_send()

    @pl.loop(1, bands)
    def _(s):
        sum_out(s).wait_send()


def on_device(
    spectrum,
    w_freq,
    b_freq,
    dilation,
    w_time,
    b_time,
    w_mix,
    ln_gain,
    w_up,
    b_up,
    w_down,
    b_down,
    epoch_lengths,
):
    channels, bins, frames = spectrum.shape
    groups = channels // SUB
    bands = lax.axis_size("band")
    blocks = lax.axis_size("tm")
    hidden = w_up.shape[1]
    epochs = epoch_lengths.shape[1]
    size = bins * bands * SUB
    some = bins // 2
    bf, f32 = jnp.bfloat16, jnp.float32
    vmem = pltpu.VMEM
    dma = pltpu.SemaphoreType.DMA
    return pl.pallas_call(
        functools.partial(kernel, bands, blocks, bins, some),
        out_shape=[jax.ShapeDtypeStruct((epochs, bins * channels), f32)] * 2,
        in_specs=[pl.BlockSpec(memory_space=vmem)] * 13,
        out_specs=[pl.BlockSpec(memory_space=vmem)] * 2,
        scratch_shapes=[
            vmem((2, channels * bins, 128), bf),
            vmem((channels * 2, frames), bf),
            vmem((channels * 2, frames), bf),
            vmem((channels * 2, frames), bf),
            vmem((channels * 2, frames), bf),
            vmem((2, 2, channels * 2, 128), bf),
            vmem((bins * SUB, frames + 2 * REACH), f32),
            vmem((groups, bands, bins * SUB, 128), bf),
            vmem((groups, size, 128), bf),
            vmem((size, size), bf),
            vmem((size, groups * 128), f32),
            vmem((bands, 2, epochs, bins * channels), f32),
            vmem((bands, 2, epochs, bins * channels), f32),
            vmem((hidden, channels), bf),
            vmem((hidden, 128), f32),
            vmem((channels, 128), f32),
            vmem((channels, 128), f32),
            vmem((epochs, 256), bf),
            dma((2, 2)),
            dma((groups, 2, 2)),
            dma((4, 2)),
            dma((groups, bands)),
            dma((groups, bands)),
            dma((groups,)),
            dma((bands,)),
            dma((bands,)),
        ],
        compiler_params=pltpu.CompilerParams(collective_id=0, has_side_effects=True),
        name="whole",
    )(
        spectrum.reshape(channels * bins, frames),
        jnp.transpose(w_freq, (0, 2, 1)),
        b_freq[None],
        dilation[None],
        w_time,
        b_time[None],
        w_mix,
        ln_gain[None],
        w_up,
        b_up[None],
        w_down.T,
        b_down[None],
        epoch_lengths,
    )


def solution(mesh):
    return jax.shard_map(
        on_device,
        mesh=mesh,
        in_specs=(
            P(None, "band", "tm"),
            P(),
            P(),
            P(),
            P(),
            P(),
            P(),
            P(),
            P(),
            P(),
            P(),
            P(),
            P("tm", None),
        ),
        out_specs=(P("tm", "band"), P("tm", "band")),
        check_vma=False,
    )
```

time: 156 us -> 81.6 us (0.52)
  the two profiles are of different devices: /device:TPU:8 before, /device:TPU:1 now
where the time goes in v3:
time: 81.6 us; the launch traced here: 81.3 us
  Pallas kernels  78 us (96%)
  local copies, waits for them, and re-layouts  2.65 us (3%)
    pallas_call x1, Pallas kernels, on_device(): pl.pallas_call(functools.partial(kernel, bands, blocks, bins, some), out_...  78 us
    unnamed x2, local copies, waits for them, and re-layouts  2.65 us

profile of v3, /device:TPU:1, one launch (start us, length us, event | category | flops | bytes accessed | tf_op | source)
XLA Modules:
  0.0 81.3 jit_solution(7845105494369031432)
XLA Ops:
  0.6 78.0 %whole.1 = (f32[8,512]{1,0:T(8,128)}, f32[8,512]{1,0:T(8,128)}) custom-call(bf16[512,2048]{1,0:T(8,128)(2,1)} %bitcast.9, bf16[5,8,64]{2,1,0:T(8,128)(2,1)} %bitcast.11, f32[1,64]{1,0:T(1,128)} %bitcast.13, s32[1,64]{1,0:T(1,128)} %bitcast.14, f32[3,64]{1,0:T(4,128)} %wtime_ref.1, f32[1,64]{1,0:T(1,128)} %bitcast.15, bf16[128,128]{1,0:T(8,128)(2,1)} %mix_ref.1, ...), custom_call_target="tpu_custom_call" | custom-call | tf_op jit(solution)/shard_map/whole/pallas_call | solution.py:489
  78.7 1.3 %copy.17 = f32[8,512]{1,0:T(8,128)} copy(f32[8,512]{1,0:T(8,128)} %get-tuple-element.4) | data formatting | bytes 32768
  80.0 1.3 %copy.18 = f32[8,512]{1,0:T(8,128)} copy(f32[8,512]{1,0:T(8,128)} %get-tuple-element.5) | data formatting | bytes 32768

commit v4 on v3

--- a/solution.py
+++ b/solution.py
@@ -14,10 +14,16 @@
 GELU_A = 0.044715
 
 
-def gelu(x):
-    inner = x * (GELU_C + (GELU_C * GELU_A) * (x * x))
-    half = 0.5 * x
-    return half + half * jnp.tanh(inner)
+def gelu_of_half(h):
+    inner = h * (2 * GELU_C + (8 * GELU_C * GELU_A) * (h * h))
+    return h + h * jnp.tanh(inner)
+
+
+def three_parts(value):
+    first = value.astype(jnp.bfloat16).astype(jnp.float32)
+    second = (value - first).astype(jnp.bfloat16).astype(jnp.float32)
+    third = (value - first - second).astype(jnp.bfloat16).astype(jnp.float32)
+    return first, second, third
 
 
 def build_kron(mix_ref, kron_ref):
@@ -59,7 +65,7 @@
     )
 
 
-def back_chunk(chunk, some, groups, data_ref, mixed_ref, up_ref, bup_ref, down_ref, bdown_ref, gain_ref, member_ref):
+def raise_chunk(chunk, half, some, groups, mixed_ref, up_ref, gain_ref, act_ref):
     channels = groups * SUB
     rows = some * SUB
     base = pl.multiple_of(chunk * rows, rows)
@@ -71,14 +77,16 @@
         var = jnp.sum(dev * dev, axis=0, keepdims=True) * (1.0 / channels)
         normed.append((dev * lax.rsqrt(var + 1e-05) * gain_ref[...]).astype(jnp.bfloat16))
     flat = jnp.concatenate(normed, axis=1)
+    flat = jnp.concatenate([flat, jnp.ones((16, some * 128), jnp.bfloat16)], axis=0)
     hidden = jnp.dot(up_ref[...], flat, preferred_element_type=jnp.float32)
-    act = jnp.concatenate(
-        [
-            gelu(hidden[:, r * 128 : (r + 1) * 128] + bup_ref[...]).astype(jnp.bfloat16)
-            for r in range(some)
-        ],
-        axis=1,
-    )
+    for r in range(some):
+        cols = slice(r * 128, (r + 1) * 128)
+        act_ref[half, :, cols] = gelu_of_half(hidden[:, cols]).astype(jnp.bfloat16)
+
+
+def lower_chunk(chunk, act, some, groups, data_ref, down_ref, bdown_ref, member_ref):
+    rows = some * SUB
+    base = pl.multiple_of(chunk * rows, rows)
     proj = jnp.dot(down_ref[...], act, preferred_element_type=jnp.float32)
     data = data_ref[:, pl.ds(base, rows), :].astype(jnp.float32)
     plain, square = [], []
@@ -119,24 +127,14 @@
     return (col == channel * bins + edge).astype(jnp.bfloat16)
 
 
-def group_weights(wt_ref, g, bins, low_on, high_on):
-    taps, size, channels = wt_ref.shape
+def weight_indices(apart_ref, place_ref, order_ref, size, bins, taps, low_on, high_on):
     long = bins + taps - 1
-    row = lax.broadcasted_iota(jnp.int32, (channels, 128), 0)
-    q = lax.broadcasted_iota(jnp.int32, (channels, 128), 1)
-    pick = ((row == g * size + q // long) & (q < size * long)).astype(jnp.bfloat16)
-    spread = [
-        jnp.dot(wt_ref[k], pick, preferred_element_type=jnp.float32) for k in range(taps)
-    ]
-    place = lax.broadcasted_iota(jnp.int32, (size, 128), 1) % long
-    base = jnp.zeros((size, 128), jnp.float32)
-    for k in range(taps):
-        base = jnp.where(place == k, spread[k], base)
-    turned = [base] + [pltpu.roll(base, f, 1) for f in range(1, bins)]
-    big = jnp.concatenate(turned, axis=0).astype(jnp.bfloat16)
-    wid = size * long
-    p = lax.broadcasted_iota(jnp.int32, (128, wid), 1)
-    src = lax.broadcasted_iota(jnp.int32, (128, wid), 0)
+    row = lax.broadcasted_iota(jnp.int32, apart_ref.shape, 0)
+    q = lax.broadcasted_iota(jnp.int32, apart_ref.shape, 1)
+    apart_ref[...] = jnp.where(q < size * long, row - q // long, -4096)
+    place_ref[...] = lax.broadcasted_iota(jnp.int32, place_ref.shape, 1) % long
+    p = lax.broadcasted_iota(jnp.int32, order_ref.shape, 1)
+    src = lax.broadcasted_iota(jnp.int32, order_ref.shape, 0)
     inner = size * bins
     lo = p - inner
     hi = lo - 2 * size
@@ -149,13 +147,30 @@
             (hi // 2) * long + bins + 2 + hi % 2 + jnp.where(high_on, 0, 4096),
         ),
     )
-    order = (src == wanted).astype(jnp.bfloat16)
-    return jnp.dot(big, order, preferred_element_type=jnp.float32).astype(jnp.bfloat16)
+    order_ref[...] = ((src == wanted) & (p < size * long)).astype(jnp.bfloat16)
+
+
+def group_weights(wt_ref, g, bins, apart_ref, place_ref, order_ref):
+    taps, size, channels = wt_ref.shape
+    wid = size * (bins + taps - 1)
+    pick = (apart_ref[...] == g * size).astype(jnp.bfloat16)
+    place = place_ref[...]
+    base = jnp.zeros((size, 128), jnp.float32)
+    for k in range(taps):
+        spread = jnp.dot(wt_ref[k], pick, preferred_element_type=jnp.float32)
+        base = jnp.where(place == k, spread, base)
+    base = 0.5 * base
+    turned = [base] + [pltpu.roll(base, f, 1) for f in range(1, bins)]
+    big = jnp.concatenate(turned, axis=0).astype(jnp.bfloat16)
+    ready = jnp.dot(big, order_ref[...], preferred_element_type=jnp.float32)
+    return ready[:, :wid].astype(jnp.bfloat16)
 
 
 def front_group(g, bands, weights, own_ref, ends_ref, low_ref, high_ref, cor_ref, rows_of, before_on, after_on, spec_ref, send_ref):
     rows = weights.shape[0]
     long = own_ref.shape[1]
+    t0, t1, t2, shift, bias8, step = (wide(column(r, g * SUB, SUB)) for r in rows_of)
+    bias = jnp.concatenate([0.5 * bias8] * (rows // SUB), axis=0)
     tiles = long // 128 + 2
     at = pl.multiple_of(g * rows, rows)
     small = pl.multiple_of(g * 16, 16)
@@ -176,12 +191,10 @@
     )
     data = jnp.concatenate([first, body, last], axis=1)
     pre = jnp.dot(weights, data, preferred_element_type=jnp.float32)
-    t0, t1, t2, shift, bias8, step = (wide(column(r, g * SUB, SUB)) for r in rows_of)
-    bias = jnp.concatenate([bias8] * (rows // SUB), axis=0)
     step = step.astype(jnp.int32)
     for j in range(tiles):
         cols = slice(j * 128, (j + 1) * 128)
-        act = gelu(pre[:, cols] + bias)
+        act = gelu_of_half(pre[:, cols] + bias)
         if j == 0:
             act = act * before_on
         if j == tiles - 1:
@@ -233,8 +246,7 @@
     down_ref,
     bdown_in,
     lens_ref,
-    mean_ref,
-    power_ref,
+    out_ref,
     ends_ref,
     plow_ref,
     phigh_ref,
@@ -249,10 +261,14 @@
     part_ref,
     got_ref,
     up_ref,
-    bup_ref,
     bdown_ref,
     gain_ref,
     member_ref,
+    apart_ref,
+    place_ref,
+    order_ref,
+    wall_ref,
+    act_ref,
     frame_sem,
     bin_sem,
     corner_sem,
@@ -359,25 +375,18 @@
         bfreq_ref[...],
         dil_ref[...].astype(jnp.float32),
     )
-    for copy in small_copies:
-        copy.wait_recv()
+    weight_indices(apart_ref, place_ref, order_ref, SUB, bins, wt_ref.shape[0], me > 0, me < bands - 1)
 
     @pl.loop(0, groups)
     def _(g):
-        weights = group_weights(wt_ref, g, bins, me > 0, me < bands - 1)
-        for copy in bin_copies(g):
-            copy.wait_recv()
-        front_group(g, bands, weights, own_ref, ends_ref, low_ref, high_ref, cor_ref, rows_of, before_on, after_on, spec_ref, send_ref)
-
-        @pl.loop(1, bands)
-        def _(s):
-            chunk_out(g, s).start()
-
-        chunk_here(g).start()
-
-    build_kron(mix_ref, kron_ref)
-    up_ref[...] = up_in[...].astype(jnp.float32).T.astype(jnp.bfloat16)
-    bup_ref[...] = wide(column(bup_in[...], 0, bup_ref.shape[0]))
+        wall_ref[g] = group_weights(wt_ref, g, bins, apart_ref, place_ref, order_ref)
+
+    sub = lax.broadcasted_iota(jnp.int32, (16, up_in.shape[1]), 0)
+    extra = jnp.zeros(sub.shape, jnp.float32)
+    for i, piece in enumerate(three_parts(bup_in[...])):
+        extra = jnp.where(sub == i, piece, extra)
+    tall = 0.5 * jnp.concatenate([up_in[...].astype(jnp.float32), extra], axis=0)
+    up_ref[...] = tall.T.astype(jnp.bfloat16)
     bdown_ref[...] = wide(column(bdown_in[...], 0, channels))
     gain_ref[...] = wide(column(gain_in[...], 0, channels))
     lens = lens_ref[...].astype(jnp.float32)
@@ -391,6 +400,23 @@
     member = jnp.where((ids >= starts) & (ids < starts + own_len), 1.0, 0.0)
     member_ref[...] = jnp.concatenate([member, member], axis=1).astype(jnp.bfloat16)
 
+    for copy in small_copies:
+        copy.wait_recv()
+
+    @pl.loop(0, groups)
+    def _(g):
+        for copy in bin_copies(g):
+            copy.wait_recv()
+        front_group(g, bands, wall_ref[g], own_ref, ends_ref, low_ref, high_ref, cor_ref, rows_of, before_on, after_on, spec_ref, send_ref)
+
+        @pl.loop(1, bands)
+        def _(s):
+            chunk_out(g, s).start()
+
+        chunk_here(g).start()
+
+    build_kron(mix_ref, kron_ref)
+
     @pl.loop(0, groups // 2)
     def _(p):
         for g in (2 * p, 2 * p + 1):
@@ -416,32 +442,38 @@
         there = lax.rem(me + bands - s, bands)
         return remote(part_ref.at[there], got_ref.at[there], sum_send.at[s], sum_recv.at[s], there, tm)
 
-    @pl.loop(1, bands + 1)
-    def _(s):
+    halves = bins // some
+
+    def raise_bins(s):
         there = lax.rem(me + s, bands)
-        for half in range(bins // some):
-            results = back_chunk(
-                there * (bins // some) + half, some, groups, data_ref, mixed_ref, up_ref, bup_ref, down_ref, bdown_ref, gain_ref, member_ref
-            )
+        for half in range(halves):
+            raise_chunk(there * halves + half, half, some, groups, mixed_ref, up_ref, gain_ref, act_ref)
+
+    def lower_bins(s, acts):
+        there = lax.rem(me + s, bands)
+        for half in range(halves):
+            results = lower_chunk(there * halves + half, acts[half], some, groups, data_ref, down_ref, bdown_ref, member_ref)
             for k in range(2):
                 part_ref[there, k, :, half * some * channels : (half + 1) * some * channels] = results[k]
 
-        @pl.when(s < bands)
-        def _():
-            sum_out(s).start()
-
-    mean_ref[...] = part_ref[me, 0]
-    power_ref[...] = part_ref[me, 1]
+    raise_bins(1)
+
+    @pl.loop(1, bands)
+    def _(s):
+        acts = [act_ref[half] for half in range(halves)]
+        lower_bins(s, acts)
+        raise_bins(s + 1)
+        sum_out(s).start()
+
+    lower_bins(bands, [act_ref[half] for half in range(halves)])
+
+    out_ref[...] = part_ref[me]
 
     @pl.loop(1, bands)
     def _(s):
         sum_in(s).wait_recv()
         there = lax.rem(me + bands - s, bands)
-        mean_ref[...] += got_ref[there, 0]
-        power_ref[...] += got_ref[there, 1]
-
-    mean_ref[...] = mean_ref[...] / own_len
-    power_ref[...] = power_ref[...] / own_len
+        out_ref[...] += got_ref[there]
 
     for copy in small_copies:
         copy.wait_send()
@@ -486,11 +518,11 @@
     bf, f32 = jnp.bfloat16, jnp.float32
     vmem = pltpu.VMEM
     dma = pltpu.SemaphoreType.DMA
-    return pl.pallas_call(
+    totals = pl.pallas_call(
         functools.partial(kernel, bands, blocks, bins, some),
-        out_shape=[jax.ShapeDtypeStruct((epochs, bins * channels), f32)] * 2,
+        out_shape=jax.ShapeDtypeStruct((2, epochs, bins * channels), f32),
         in_specs=[pl.BlockSpec(memory_space=vmem)] * 13,
-        out_specs=[pl.BlockSpec(memory_space=vmem)] * 2,
+        out_specs=pl.BlockSpec(memory_space=vmem),
         scratch_shapes=[
             vmem((2, channels * bins, 128), bf),
             vmem((channels * 2, frames), bf),
@@ -505,11 +537,15 @@
             vmem((size, groups * 128), f32),
             vmem((bands, 2, epochs, bins * channels), f32),
             vmem((bands, 2, epochs, bins * channels), f32),
-            vmem((hidden, channels), bf),
-            vmem((hidden, 128), f32),
+            vmem((hidden, channels + 16), bf),
             vmem((channels, 128), f32),
             vmem((channels, 128), f32),
             vmem((epochs, 256), bf),
+            vmem((channels, 128), jnp.int32),
+            vmem((SUB, 128), jnp.int32),
+            vmem((128, 128), bf),
+            vmem((groups, bins * SUB, SUB * (bins + 4)), bf),
+            vmem((2, hidden, some * 128), bf),
             dma((2, 2)),
             dma((groups, 2, 2)),
             dma((4, 2)),
@@ -536,6 +572,8 @@
         b_down[None],
         epoch_lengths,
     )
+    lens = epoch_lengths[0].astype(f32)[:, None]
+    return totals[0] / lens, totals[1] / lens
 
 
 def solution(mesh):

time: 81.6 us -> 77.4 us (0.949)
  Pallas kernels: 78 us -> 74.5 us
  local copies, waits for them, and re-layouts: 2.65 us -> 0 us
  other arithmetic: 0 us -> 2.08 us
    pallas_call x1, Pallas kernels: 78 us -> 74.5 us  [on_device(): pl.pallas_call(functools.partial(kernel, bands, blocks, bins, some), out_...]
    unnamed x2 -> x0, local copies, waits for them, and re-layouts: 2.65 us -> none
    div x0 -> x1, other arithmetic: none -> 1.42 us  [on_device(): return (totals[0] / lens, totals[1] / lens)]
where the time goes in v4:
time: 77.4 us; the launch traced here: 77.2 us
  Pallas kernels  74.5 us (96%)
  other arithmetic  2.08 us (3%)
    pallas_call x1, Pallas kernels, on_device(): pl.pallas_call(functools.partial(kernel, bands, blocks, bins, some), out_...  74.5 us

profile of v4, /device:TPU:1, one launch (start us, length us, event | category | flops | bytes accessed | tf_op | source)
XLA Modules:
  0.0 77.2 jit_solution(1072497399199389232)
XLA Ops:
  0.6 0.7 convert_bitcast_fusion
  1.3 74.5 %whole.1 = f32[2,8,512]{2,1,0:T(8,128)} custom-call(bf16[512,2048]{1,0:T(8,128)(2,1)} %bitcast.15, bf16[5,8,64]{2,1,0:T(8,128)(2,1)} %bitcast.17, f32[1,64]{1,0:T(1,128)} %bitcast.19, s32[1,64]{1,0:T(1,128)} %bitcast.20, f32[3,64]{1,0:T(4,128)} %wtime_ref.1, f32[1,64]{1,0:T(1,128)} %bitcast.21, bf16[128,128]{1,0:T(8,128)(2,1)} %mix_ref.1, f32[1,64]{1,0:T(1,128)} %bitcast.22, ...), custom_call_target="tpu_custom_call" | custom-call | tf_op jit(solution)/shard_map/whole/pallas_call | solution.py:521
  75.8 1.4 %bitcast_divide_fusion = (f32[8,512]{1,0:T(8,128)}, f32[8,512]{1,0:T(8,128)}) fusion(f32[2,8,512]{2,1,0:T(8,128)} %whole.1, f32[8]{0:T(128)S(1)} %convert_bitcast_fusion), kind=kLoop, calls=%fused_computation | loop fusion | flops 8192 | bytes 65568 | tf_op jit(solution)/shard_map/div | solution.py:576

commit v5 on v4

--- a/solution.py
+++ b/solution.py
@@ -16,6 +16,11 @@
 
 def gelu_of_half(h):
     inner = h * (2 * GELU_C + (8 * GELU_C * GELU_A) * (h * h))
+    return h + h * jnp.tanh(inner)
+
+
+def gelu_of_half_narrow(h):
+    inner = h * (jnp.bfloat16(2 * GELU_C) + jnp.bfloat16(8 * GELU_C * GELU_A) * (h * h))
     return h + h * jnp.tanh(inner)
 
 
@@ -65,7 +70,7 @@
     )
 
 
-def raise_chunk(chunk, half, some, groups, mixed_ref, up_ref, gain_ref, act_ref):
+def norm_chunk(chunk, some, groups, mixed_ref, gain_ref):
     channels = groups * SUB
     rows = some * SUB
     base = pl.multiple_of(chunk * rows, rows)
@@ -77,17 +82,19 @@
         var = jnp.sum(dev * dev, axis=0, keepdims=True) * (1.0 / channels)
         normed.append((dev * lax.rsqrt(var + 1e-05) * gain_ref[...]).astype(jnp.bfloat16))
     flat = jnp.concatenate(normed, axis=1)
-    flat = jnp.concatenate([flat, jnp.ones((16, some * 128), jnp.bfloat16)], axis=0)
+    return jnp.concatenate([flat, jnp.ones((16, some * 128), jnp.bfloat16)], axis=0)
+
+
+def raise_chunk(flat, half, some, up_ref, act_ref):
     hidden = jnp.dot(up_ref[...], flat, preferred_element_type=jnp.float32)
     for r in range(some):
         cols = slice(r * 128, (r + 1) * 128)
-        act_ref[half, :, cols] = gelu_of_half(hidden[:, cols]).astype(jnp.bfloat16)
-
-
-def lower_chunk(chunk, act, some, groups, data_ref, down_ref, bdown_ref, member_ref):
+        act_ref[half, :, cols] = gelu_of_half_narrow(hidden[:, cols].astype(jnp.bfloat16))
+
+
+def lower_chunk(chunk, proj, some, groups, data_ref, bdown_ref, member_ref):
     rows = some * SUB
     base = pl.multiple_of(chunk * rows, rows)
-    proj = jnp.dot(down_ref[...], act, preferred_element_type=jnp.float32)
     data = data_ref[:, pl.ds(base, rows), :].astype(jnp.float32)
     plain, square = [], []
     for r in range(some):
@@ -444,28 +451,37 @@
 
     halves = bins // some
 
-    def raise_bins(s):
-        there = lax.rem(me + s, bands)
-        for half in range(halves):
-            raise_chunk(there * halves + half, half, some, groups, mixed_ref, up_ref, gain_ref, act_ref)
-
-    def lower_bins(s, acts):
-        there = lax.rem(me + s, bands)
-        for half in range(halves):
-            results = lower_chunk(there * halves + half, acts[half], some, groups, data_ref, down_ref, bdown_ref, member_ref)
-            for k in range(2):
-                part_ref[there, k, :, half * some * channels : (half + 1) * some * channels] = results[k]
-
-    raise_bins(1)
+    def chunk_of(s, half):
+        return lax.rem(me + s, bands) * halves + half
+
+    def norms(s):
+        return [norm_chunk(chunk_of(s, half), some, groups, mixed_ref, gain_ref) for half in range(halves)]
+
+    def downs():
+        return [
+            jnp.dot(down_ref[...], act_ref[half], preferred_element_type=jnp.float32)
+            for half in range(halves)
+        ]
+
+    def lower_half(s, half, proj):
+        results = lower_chunk(chunk_of(s, half), proj, some, groups, data_ref, bdown_ref, member_ref)
+        for k in range(2):
+            part_ref[lax.rem(me + s, bands), k, :, half * some * channels : (half + 1) * some * channels] = results[k]
+
+    for half, flat in enumerate(norms(1)):
+        raise_chunk(flat, half, some, up_ref, act_ref)
 
     @pl.loop(1, bands)
     def _(s):
-        acts = [act_ref[half] for half in range(halves)]
-        lower_bins(s, acts)
-        raise_bins(s + 1)
+        projs = downs()
+        flats = norms(s + 1)
+        for half in range(halves):
+            lower_half(s, half, projs[half])
+            raise_chunk(flats[half], half, some, up_ref, act_ref)
         sum_out(s).start()
 
-    lower_bins(bands, [act_ref[half] for half in range(halves)])
+    for half, proj in enumerate(downs()):
+        lower_half(bands, half, proj)
 
     out_ref[...] = part_ref[me]
 

time: 77.4 us -> 73.4 us (0.948)
  Pallas kernels: 74.5 us -> 70.5 us
    pallas_call x1, Pallas kernels: 74.5 us -> 70.5 us  [on_device(): pl.pallas_call(functools.partial(kernel, bands, blocks, bins, some), out_...]
where the time goes in v5:
time: 73.4 us; the launch traced here: 73.2 us
  Pallas kernels  70.5 us (96%)
  other arithmetic  2.08 us (3%)
    pallas_call x1, Pallas kernels, on_device(): pl.pallas_call(functools.partial(kernel, bands, blocks, bins, some), out_...  70.5 us

profile of v5, /device:TPU:1, one launch (start us, length us, event | category | flops | bytes accessed | tf_op | source)
XLA Modules:
  0.0 73.2 jit_solution(4647719161965363449)
XLA Ops:
  0.6 0.7 convert_bitcast_fusion
  1.3 70.5 %whole.1 = f32[2,8,512]{2,1,0:T(8,128)} custom-call(bf16[512,2048]{1,0:T(8,128)(2,1)} %bitcast.15, bf16[5,8,64]{2,1,0:T(8,128)(2,1)} %bitcast.17, f32[1,64]{1,0:T(1,128)} %bitcast.19, s32[1,64]{1,0:T(1,128)} %bitcast.20, f32[3,64]{1,0:T(4,128)} %wtime_ref.1, f32[1,64]{1,0:T(1,128)} %bitcast.21, bf16[128,128]{1,0:T(8,128)(2,1)} %mix_ref.1, f32[1,64]{1,0:T(1,128)} %bitcast.22, ...), custom_call_target="tpu_custom_call" | custom-call | tf_op jit(solution)/shard_map/whole/pallas_call | solution.py:537
  71.8 1.4 %bitcast_divide_fusion = (f32[8,512]{1,0:T(8,128)}, f32[8,512]{1,0:T(8,128)}) fusion(f32[2,8,512]{2,1,0:T(8,128)} %whole.1, f32[8]{0:T(128)S(1)} %convert_bitcast_fusion), kind=kLoop, calls=%fused_computation | loop fusion | flops 8192 | bytes 65568 | tf_op jit(solution)/shard_map/div | solution.py:592

commit v6 on v5

--- a/solution.py
+++ b/solution.py
@@ -417,8 +417,9 @@
         front_group(g, bands, wall_ref[g], own_ref, ends_ref, low_ref, high_ref, cor_ref, rows_of, before_on, after_on, spec_ref, send_ref)
 
         @pl.loop(1, bands)
-        def _(s):
-            chunk_out(g, s).start()
+        def _(k):
+            step = (k // 2) * (2 * (k % 2) - 1)
+            chunk_out(g, bands // 2 + step).start()
 
         chunk_here(g).start()
 
@@ -490,6 +491,8 @@
         sum_in(s).wait_recv()
         there = lax.rem(me + bands - s, bands)
         out_ref[...] += got_ref[there]
+
+    out_ref[...] = out_ref[...] / own_len
 
     for copy in small_copies:
         copy.wait_send()
@@ -588,8 +591,7 @@
         b_down[None],
         epoch_lengths,
     )
-    lens = epoch_lengths[0].astype(f32)[:, None]
-    return totals[0] / lens, totals[1] / lens
+    return totals[0], totals[1]
 
 
 def solution(mesh):

time: 73.4 us -> 72.4 us (0.986)
  other arithmetic: 2.08 us -> 0 us
  local copies, waits for them, and re-layouts: 0 us -> 1.35 us
    div x1 -> x0, other arithmetic: 1.42 us -> none  [on_device(): return (totals[0] / lens, totals[1] / lens)]
    squeeze x0 -> x1, local copies, waits for them, and re-layouts: none -> 1.35 us  [on_device(): return (totals[0], totals[1])]
where the time goes in v6:
time: 72.4 us; the launch traced here: 72.1 us
  Pallas kernels  70.1 us (97%)
  local copies, waits for them, and re-layouts  1.35 us (2%)
    pallas_call x1, Pallas kernels, on_device(): pl.pallas_call(functools.partial(kernel, bands, blocks, bins, some), out_...  70.1 us

profile of v6, /device:TPU:1, one launch (start us, length us, event | category | flops | bytes accessed | tf_op | source)
XLA Modules:
  0.0 72.1 jit_solution(13478644322139747617)
XLA Ops:
  0.6 70.1 %whole.1 = f32[2,8,512]{2,1,0:T(8,128)} custom-call(bf16[512,2048]{1,0:T(8,128)(2,1)} %bitcast.13, bf16[5,8,64]{2,1,0:T(8,128)(2,1)} %bitcast.15, f32[1,64]{1,0:T(1,128)} %bitcast.17, s32[1,64]{1,0:T(1,128)} %bitcast.18, f32[3,64]{1,0:T(4,128)} %wtime_ref.1, f32[1,64]{1,0:T(1,128)} %bitcast.19, bf16[128,128]{1,0:T(8,128)(2,1)} %mix_ref.1, f32[1,64]{1,0:T(1,128)} %bitcast.20, ...), custom_call_target="tpu_custom_call" | custom-call | tf_op jit(solution)/shard_map/whole/pallas_call | solution.py:540
  70.8 1.3 %slice_bitcast_fusion = (f32[8,512]{1,0:T(8,128)}, f32[8,512]{1,0:T(8,128)}) fusion(f32[2,8,512]{2,1,0:T(8,128)} %whole.1), kind=kLoop, calls=%fused_computation | loop fusion | bytes 65536 | tf_op jit(solution)/shard_map/squeeze | solution.py:594
